TPU v7x, 256 devices: a whole 4x4x8 slice. The times are simulated.
256 devices in a mesh: seq: 32 (over y, z_lo, core), head: 8 (over x, z_hi).
Axes of the slice: x: 4, y: 4, z: 8 (z_hi: 2, z_lo: 4; z = z_hi * 4 + z_lo), core: 2. Of those that a mesh axis runs over, the one named last changes fastest.
Arguments:
- queries: bfloat16 [4096, 8192], P('seq', 'head'), may hold values from -48 to 48
- keyval: bfloat16 [4096, 2048], P('seq', 'head'), may hold values from -48 to 48
- grad_out: bfloat16 [4096, 8192], P('seq', 'head'), may hold values from -6 to 6
- doc_ids: int32 [4096], P('seq'), may hold values from 0 to 3, never falling along the last dimension, each value on 1 to 2048 neighbouring positions
- deltas: bfloat16 [8, 4096, 8192], P('head', 'seq'), may hold values from -6 to 6
- node_weights: bfloat16 [8192, 2048], P('head', 'seq'), may hold values from -0.0625 to 0.0625
- layer_slot: int32 [8], replicated, may hold values from 0 to 7, each once
Outputs:
- grad_query: bfloat16 [4096, 8192], P('seq', 'head')
- grad_keyval: bfloat16 [4096, 2048], P('seq', 'head')
- scores: float32 [8, 16], replicated
Inputs may be any that keep to these rules, and one draw needn't show every extreme that they name: `layer_slot`: each of the 8 layers stands in exactly one slot. `doc_ids`: never falling along the sequence.
All inputs are finite; a program needn't handle non-finite values.
Results may differ from a plain program's by a relative error of at most 0.013.
Values may be sent and summed in bfloat16 or wider, within the bound.
A program may use at most 64 MiB of HBM per device.

v0:
```python
import math

import jax
import jax.numpy as jnp
from jax import lax
from jax.sharding import PartitionSpec as P

H = 64
KVH = 8
HD = 128


def over_blocks(step, carry, pieces):
    total_rows = pieces[0].shape[0]
    block_rows = 512

    def one_turn(turn_index, running):
        offset = turn_index * block_rows
        blocks = tuple((lax.dynamic_slice_in_dim(piece, offset, block_rows, 0) for piece in pieces))
        return step(running, *blocks, offset)

    return lax.fori_loop(0, total_rows // block_rows, one_turn, carry)


def on_device(queries, keyval, grad_out, doc_ids, deltas, node_weights, layer_slot):
    tok_rows = queries.shape[0]
    kv_local = keyval.shape[1] // (2 * HD)
    group_size = H // KVH
    score_scale = 1.0 / math.sqrt(HD)
    seq_total = tok_rows * lax.axis_size("seq")
    query_grid = queries.reshape(tok_rows, kv_local, group_size, HD)
    out_grid = grad_out.reshape(tok_rows, kv_local, group_size, HD)
    row_positions = lax.axis_index("seq") * tok_rows + jnp.arange(tok_rows, dtype=jnp.int32)

    def block_logits(kv_rows, key_ids, key_start):
        width = kv_rows.shape[0]
        kv_grid = kv_rows.reshape(width, kv_local, 2, HD)
        logits = (
            jnp.einsum(
                "tgie,rge->gitr", query_grid, kv_grid[:, :, 0], preferred_element_type=jnp.float32
            )
            * score_scale
        )
        key_positions = key_start + jnp.arange(width, dtype=jnp.int32)
        allowed = (key_ids[None, :] == doc_ids[:, None]) & (
            key_positions[None, :] <= row_positions[:, None]
        )
        return (logits, allowed, kv_grid)

    def forward_step(carry, kv_rows, key_ids, key_start):
        run_max, run_sum, accum = carry
        logits, allowed, kv_grid = block_logits(kv_rows, key_ids, key_start)
        new_max = jnp.maximum(run_max, jnp.max(jnp.where(allowed, logits, -1e30), axis=3))
        weights = jnp.where(allowed, jnp.exp(logits - new_max[..., None]), 0.0)
        factor = jnp.exp(run_max - new_max)
        run_sum = run_sum * factor + jnp.sum(weights, axis=3)
        values = kv_grid[:, :, 1].astype(jnp.float32)
        accum = accum * factor[..., None] + jnp.einsum(
            "gitr,rge->gite", weights, values, precision=lax.Precision.HIGHEST
        )
        return (new_max, run_sum, accum)

    stat_shape = (kv_local, group_size, tok_rows)
    forward_init = (
        jnp.full(stat_shape, -1e30, jnp.float32),
        jnp.zeros(stat_shape, jnp.float32),
        jnp.zeros(stat_shape + (HD,), jnp.float32),
    )
    run_max, run_sum, accum = over_blocks(
        forward_step,
        forward_init,
        (
            lax.all_gather(keyval, "seq", axis=0, tiled=True),
            lax.all_gather(doc_ids, "seq", axis=0, tiled=True),
        ),
    )
    log_total = run_max + jnp.log(run_sum)
    attn_out = accum / run_sum[..., None]
    row_dot = jnp.einsum(
        "tgie,gite->git", out_grid.astype(jnp.float32), attn_out, precision=lax.Precision.HIGHEST
    )

    def backward_step(carry, kv_rows, key_ids, key_start):
        query_accum = carry[0]
        width = kv_rows.shape[0]
        logits, allowed, kv_grid = block_logits(kv_rows, key_ids, key_start)
        probs = jnp.where(allowed, jnp.exp(logits - log_total[..., None]), 0.0)
        grad_probs = jnp.einsum(
            "tgie,rge->gitr", out_grid, kv_grid[:, :, 1], preferred_element_type=jnp.float32
        )
        grad_logits = (probs * (grad_probs - row_dot[..., None])).astype(jnp.bfloat16)
        query_accum = (
            query_accum
            + jnp.einsum(
                "gitr,rge->gite", grad_logits, kv_grid[:, :, 0], preferred_element_type=jnp.float32
            )
            * score_scale
        )
        probs_low = probs.astype(jnp.bfloat16)
        grad_keys = (
            jnp.einsum(
                "gitr,tgie->rge", grad_logits, query_grid, preferred_element_type=jnp.float32
            )
            * score_scale
        )
        grad_values = jnp.einsum(
            "gitr,tgie->rge", probs_low, out_grid, preferred_element_type=jnp.float32
        )
        block_grad = jnp.stack((grad_keys, grad_values), axis=2).reshape(width, kv_local * 2 * HD)
        kv_buffer = lax.dynamic_update_slice(
            carry[1], block_grad, (key_start, jnp.zeros((), jnp.int32))
        )
        return (query_accum, kv_buffer)

    query_zero = jnp.zeros(stat_shape + (HD,), jnp.float32)
    backward_init = (query_zero, jnp.zeros((seq_total, kv_local * 2 * HD), jnp.float32))
    backward_out = over_blocks(
        backward_step,
        backward_init,
        (
            lax.all_gather(keyval, "seq", axis=0, tiled=True),
            lax.all_gather(doc_ids, "seq", axis=0, tiled=True),
        ),
    )
    query_accum = backward_out[0]
    grad_query = (
        jnp.transpose(query_accum, (2, 0, 1, 3))
        .reshape(tok_rows, kv_local * group_size * HD)
        .astype(jnp.bfloat16)
    )
    grad_keyval = lax.psum_scatter(
        backward_out[1].astype(jnp.bfloat16), "seq", scatter_dimension=0, tiled=True
    )
    width_deltas = lax.all_to_all(deltas, "head", split_axis=2, concat_axis=0, tiled=True)
    grad_rows = lax.all_gather(grad_keyval, "head", axis=1, tiled=True)
    layer_count = width_deltas.shape[0]
    node_count = grad_rows.shape[1] // HD
    projected = jnp.einsum(
        "ltd,dc->ltc",
        width_deltas,
        lax.all_gather(node_weights, "seq", axis=1, tiled=True),
        preferred_element_type=jnp.float32,
    )
    grad_cols = grad_rows.astype(jnp.float32)
    per_column = jnp.sum(projected * grad_cols[None], axis=1)
    partial_value = jnp.sum(per_column.reshape(layer_count, node_count, HD), axis=2)
    totals = lax.psum(partial_value / math.sqrt(seq_total), ("seq", "head"))
    placing = (layer_slot[:, None] == jnp.arange(layer_count, dtype=jnp.int32)[None, :]).astype(
        jnp.float32
    )
    scores = jnp.dot(placing.T, totals, precision=lax.Precision.HIGHEST)
    return (grad_query, grad_keyval, scores)


def solution(mesh):
    return jax.shard_map(
        on_device,
        mesh=mesh,
        in_specs=(
            P("seq", "head"),
            P("seq", "head"),
            P("seq", "head"),
            P("seq"),
            P("head", "seq", None),
            P("head", "seq"),
            P(),
        ),
        out_specs=(P("seq", "head"), P("seq", "head"), P()),
        check_vma=False,
    )
```

profile of v0, /device:TPU:8, one launch (start us, length us, event | category | flops | bytes accessed | tf_op | source)
XLA Modules:
  0.0 490.0 jit_solution(3479772316284741002)
XLA Ops:
  13.7 37.6 %all-gather = s32[32,1,128]{2,1,0:T(1,128)S(1)} all-gather(s32[1,1,128]{2,1,0:T(1,128)S(1)} %bitcast.262), channel_id=1, replica_groups=mesh['seq'=32,'head'=8] {'seq'}, dimensions={0}, use_global_device_ids=true | all-gather | bytes 16896 | tf_op jit(solution)/shard_map/all_gather | solution.py:122
  51.3 25.2 %all-gather.4.cloned.1.call-done = bf16[4096,256]{0,1:T(8,128)(2,1)} async-done(((bf16[128,256]{0,1:T(8,128)(2,1)}), bf16[4096,256]{0,1:T(8,128)(2,1)}) %all-gather.4.cloned.1.call-update) | async-done | bytes 2097168 | tf_op jit(solution)/shard_map/all_gather | solution.py:121
  76.6 55.1 %while.34 = (s32[]{:T(128)}, f32[1,8,128]{2,1,0:T(8,128)S(1)}, f32[1,8,128]{2,1,0:T(8,128)S(1)}, f32[1,8,128,128]{3,2,1,0:T(8,128)}, s32[4096]{0:T(1024)S(1)}, /...) while((s32[]{:T(128)}, f32[1,8,128]{2,1,0:T(8,128)S(1)}, ...), condition=%wide.region_3.4_spmd.clone, body=%wide.region_0.3_spmd.clone.sunk | while | flops 945363584 | bytes 8728263 | solution.py:22
  79.3 2.8 fusion.70
  85.3 3.8 fusion.70
  92.3 3.8 fusion.70
  99.3 3.8 fusion.70
  106.3 3.8 fusion.70
  113.3 3.8 fusion.70
  120.4 3.8 fusion.70
  127.4 3.8 fusion.70
  135.9 39.6 %while.35 = (s32[]{:T(128)}, f32[1,8,128,128]{3,2,1,0:T(8,128)S(1)}, bf16[4096,256]{1,0:T(8,128)(2,1)}, s32[4096]{0:T(1024)S(1)}, s32[128]{0:T(128)S(1)}, /*inde...) while((s32[]{:T(128)}, ...), condition=%wide.region_5.6_spmd.clone, body=%wide.region_4.5_spmd.clone.sunk | while | flops 675611264 | bytes 14438105 | solution.py:22
  177.1 6.9 %copy.73 = bf16[1,128,8192]{1,0,2:T(2,128)(2,1)} copy(bf16[1,128,8192]{2,1,0:T(8,128)(2,1)S(1)} %copy-done) | data formatting | bytes 4194304 | tf_op args[4]
  184.4 45.2 %reduce.8 = bf16[8192,128]{1,0:T(8,128)(2,1)S(1)} reduce(bf16[8192,1,128]{2,1,0:T(2,128)(2,1)} %bitcast.245, bf16[]{:T(256)} %broadcast.122), dimensions={1}, to_apply=%bitcast.163.reduce_sub_computation | reduce | bytes 4194306
  229.6 3.2 reshape.216
  232.9 58.4 %all_to_all.18 = bf16[8,2,65536]{2,1,0:T(2,128)(2,1)S(1)} all-to-all(bf16[8,2,65536]{2,1,0:T(2,128)(2,1)} %reshape.216), channel_id=1, replica_groups=mesh['seq'=32,'head'=8] {'head'}, dimensions={0} | all-to-all | bytes 4194304 | tf_op jit(solution)/shard_map/all_to_all | solution.py:134
  291.3 4.4 reshape.217
  295.7 2.5 copy.93
  298.2 2.6 copy.74
  301.8 17.4 %reduce-scatter.2.cloned.1.call-done = bf16[128,256]{1,0:T(8,128)(2,1)} async-done(((bf16[4096,256]{1,0:T(8,128)(2,1)}), bf16[128,256]{1,0:T(8,128)(2,1)}) %reduce-scatter.2.cloned.1.call-update) | async-done | bytes 65552 | tf_op jit(solution)/shard_map/reduce_scatter | solution.py:131
  319.2 47.9 %all_gather.17 = bf16[128,2048]{1,0:T(8,128)(2,1)S(1)} all-gather(bf16[128,256]{1,0:T(8,128)(2,1)} %reduce-scatter.2.cloned.1.call-done), channel_id=1, replica_groups=mesh['seq'=32,'head'=8] {'head'}, dimensions={1}, use_global_device_ids=true | all-gather | bytes 589824 | tf_op jit(solution)/shard_map/all_gather | solution.py:135
  368.2 31.0 %all-gather.6.cloned.1.call-done = bf16[1024,2048]{0,1:T(8,128)(2,1)} async-done(((bf16[1024,64]{0,1:T(8,128)(2,1)}), bf16[1024,2048]{0,1:T(8,128)(2,1)}) %all-gather.6.cloned.1.call-update) | async-done | bytes 4194320 | tf_op jit(solution)/shard_map/all_gather | solution.py:141
  399.2 7.2 %multiply_reduce_fusion = f32[8,2048]{1,0:T(8,128)S(1)} fusion(bf16[1024,2048]{0,1:T(8,128)(2,1)} %all-gather.6.cloned.1.call-done, f32[128,2048]{1,0:T(8,128)} %convert_element_type.38, bf16[1,128,8,1024]{3,1,2,0:T(8,128)(2,1)S(1)} %copy-done.1), kind=kOutput, calls=%fused_computation.60 | convolution fusion | flops 4299145216 | bytes 7405568 | tf_op jit(solution)/shard_map/ltd,dc->ltc/dot_general | solution.py:138
  406.5 76.2 %psum.7 = f32[8,16]{0,1:T(8,128)S(1)} all-reduce(f32[8,16]{0,1:T(8,128)S(1)} %broadcast_multiply_fusion), channel_id=1, replica_groups=mesh['seq'=32,'head'=8] {'seq','head'}, use_global_device_ids=true, to_apply=%region_9.10 | all-reduce | flops 128 | bytes 1024 | tf_op jit(solution)/shard_map/psum | solution.py:147
  (220 shorter events, 79.9 us)
Async XLA Ops:
  7.2 6.6 %copy-start.2 = (s32[128]{0:T(128)S(1)}, s32[128]{0:T(128)}, u32[]{:S(2)}) copy-start(s32[128]{0:T(128)} %param.14) | copy-start | bytes 1540
  7.2 69.4 %all-gather.4.cloned.1.call-start = ((), (), s32[]{:S(2)}) async-start(), calls=%async_computation.2 | async-start | bytes 2162688 | tf_op jit(solution)/shard_map/all_gather | solution.py:121
  8.8 310.4 %reduce-scatter.2.cloned.1.call-start = ((), (), s32[]{:S(2)}) async-start(), calls=%async_computation.3 | async-start | bytes 2162688 | tf_op jit(solution)/shard_map/reduce_scatter | solution.py:131
  175.5 1.6 copy-start
  175.5 223.7 %all-gather.6.cloned.1.call-start = ((), (), s32[]{:S(2)}) async-start(), calls=%async_computation.4 | async-start | bytes 4325376 | tf_op jit(solution)/shard_map/all_gather | solution.py:141
  300.8 98.4 %copy-start.1 = (bf16[1,128,8,1024]{3,1,2,0:T(8,128)(2,1)S(1)}, bf16[1,128,8,1024]{3,1,2,0:T(8,128)(2,1)}, u32[]{:S(2)}) copy-start(bf16[1,128,8,1024]{3,1,2,0:T(8,128)(2,1)} %copy.74) | copy-start | bytes 6291460
  368.2 114.4 %copy-start.3 = (s32[8]{0:T(128)S(1)}, s32[8]{0:T(128)}, u32[]{:S(2)}) copy-start(s32[8]{0:T(128)} %param.17) | copy-start | bytes 100
Sparse Core Ops, SparseCore 0:
  10.3 66.1 all-gather.3
  175.6 143.5 reduce-scatter.1
  321.1 78.0 all-gather.5
where the time goes:
time: 493 us; the launch traced here: 490 us
  blocking collectives  220 us (45%)
  waiting for transfers between devices  74.2 us (15%)
  matrix products  70.4 us (14%)
  other arithmetic  56.2 us (11%)
  local copies, waits for them, and re-layouts  53.7 us (11%)
  between operations  13.9 us (3%)
    psum x1, blocking collectives, on_device(): totals = lax.psum(partial_value / math.sqrt(seq_total), ('seq', 'head'))  76.2 us
    all_to_all x1, blocking collectives, on_device(): lax.all_to_all(deltas, 'head', split_axis=2, concat_axis=0, tiled=True)  58.4 us
    all_gather x1, blocking collectives, on_device(): grad_rows = lax.all_gather(grad_keyval, 'head', axis=1, tiled=True)  47.9 us
    unnamed x6, other arithmetic  46.5 us
    all_gather x1, blocking collectives, on_device(): lax.all_gather(doc_ids, 'seq', axis=0, tiled=True)  37.6 us
    all_gather x1, waiting for transfers between devices, on_device(): lax.all_gather(node_weights, 'seq', axis=1, tiled=True)  31 us
    dot_general x8, matrix products, forward_step(): jnp.einsum('gitr,rge->gite', weights, values, precision=lax.Precision.HIG...  29.4 us
    unnamed x19, local copies, waits for them, and re-layouts  25.4 us
  transfers between devices with their start and end apart: 3, of which 3 were waited for; matrix products, arithmetic and copies ran while one was open for 15% of the time, Pallas kernels for 0%

commit v1 on v0

v1 whole, which is shorter than its diff:
```python
import math

import jax
import jax.numpy as jnp
from jax import lax
from jax.experimental import pallas as pl
from jax.experimental.pallas import tpu as pltpu
from jax.sharding import PartitionSpec as P

HD = 128
GROUP = 8
ROWS = 128
SPAN = 9
NEG = -1e30
FLOOR = -1e29
SCALE = 1.0 / math.sqrt(HD)
EXP_SCALE = SCALE * math.log2(math.e)
MESH = pl.DeviceIdType.MESH
NT = (((1,), (1,)), ((), ()))


def remote(src, dst, send, recv, seq, head):
    return pltpu.make_async_remote_copy(
        src_ref=src,
        dst_ref=dst,
        send_sem=send,
        recv_sem=recv,
        device_id=(seq, head),
        device_id_type=MESH,
    )


def kernel(
    q_ref,
    kv_ref,
    go_ref,
    doc_ref,
    del_ref,
    wt_ref,
    gq_ref,
    gkv_ref,
    sc_ref,
    q8,
    go8,
    kvbuf,
    docbuf,
    docq,
    bias,
    ebuf,
    dpbuf,
    mxb,
    lsb,
    dsb,
    stat,
    strecv,
    pbuf,
    dsbuf,
    sendbuf,
    dkvrecv,
    ownbuf,
    dqbuf,
    dqrecv,
    dbuf,
    wbuf,
    pbig,
    gbuf,
    arsrc,
    ar1,
    ar2,
    ar3,
    kvs,
    kvr,
    docs,
    docr,
    qs,
    qr,
    sts,
    str_,
    dks,
    dkr,
    dqs,
    dqr,
    dls,
    dlr,
    loc,
    ays,
    ayr,
    azps,
    azpr,
    azms,
    azmr,
    bzps,
    bzpr,
    bzms,
    bzmr,
    bys,
    byr,
    fas,
    far,
    fbs,
    fbr,
    g1s,
    g1r,
    gxs,
    gxr,
    a1s,
    a1r,
    a2s,
    a2r,
    a3s,
    a3r,
):
    s = lax.axis_index("seq")
    h = lax.axis_index("head")
    core = lax.rem(s, 2)
    chip = s // 2
    zl = lax.rem(chip, 4)
    y = chip // 4
    zh = lax.rem(h, 2)
    x = h // 2
    z = zh * 4 + zl
    sib = s + 1 - 2 * core

    def at_yz(y_, z_, c_):
        return (y_ * 4 + lax.rem(z_, 4)) * 2 + c_, x * 2 + z_ // 4

    def kv_copy(j):
        return remote(kv_ref, kvbuf.at[j], kvs.at[j], kvr.at[j], lax.rem(s + 2 * j, 32), h)

    def doc_copy(j):
        return remote(doc_ref, docbuf.at[j], docs.at[j], docr.at[j], lax.rem(s + 2 * j, 32), h)

    def q_copy(g):
        return remote(
            q_ref.at[:, pl.ds(g * HD, HD)],
            q8.at[g, pl.ds(core * ROWS, ROWS)],
            qs.at[g],
            qr.at[g],
            sib,
            h,
        )

    def go_copy(g):
        return remote(
            go_ref.at[:, pl.ds(g * HD, HD)],
            go8.at[g, pl.ds(core * ROWS, ROWS)],
            qs.at[8 + g],
            qr.at[8 + g],
            sib,
            h,
        )

    def q_wait(g):
        return remote(
            q_ref.at[:, pl.ds(g * HD, HD)],
            q8.at[g, pl.ds((1 - core) * ROWS, ROWS)],
            qs.at[g],
            qr.at[g],
            sib,
            h,
        )

    def go_wait(g):
        return remote(
            go_ref.at[:, pl.ds(g * HD, HD)],
            go8.at[g, pl.ds((1 - core) * ROWS, ROWS)],
            qs.at[8 + g],
            qr.at[8 + g],
            sib,
            h,
        )

    docq_send = remote(doc_ref, docq.at[core], docs.at[0], docr.at[0], sib, h)
    docq_wait = remote(doc_ref, docq.at[1 - core], docs.at[0], docr.at[0], sib, h)
    docq_send.start()
    for g in range(GROUP):
        q_copy(g).start()
        go_copy(g).start()
    for j in range(1, SPAN):

        @pl.when(chip + j <= 15)
        def _():
            doc_copy(j).start()
            kv_copy(j).start()

    def del_copy(k):
        xt = lax.rem(x + k, 4)
        return remote(
            del_ref.at[:, pl.ds(xt * 2048, 2048)],
            dbuf.at[x],
            dls.at[k],
            dlr.at[k],
            s,
            xt * 2 + zh,
        )

    def del_wait(k):
        xf = lax.rem(x + 4 - k, 4)
        return remote(
            del_ref.at[:, pl.ds(xf * 2048, 2048)],
            dbuf.at[xf],
            dls.at[k],
            dlr.at[k],
            s,
            xf * 2 + zh,
        )

    for k in range(1, 4):
        del_copy(k).start()
    own_delta = pltpu.make_async_copy(
        del_ref.at[:, pl.ds(x * 2048, 2048)], dbuf.at[x], loc.at[0]
    )
    own_delta.start()

    LO, HI = pl.ds(0, 512), pl.ds(512, 512)
    own_w = pltpu.make_async_copy(wt_ref, wbuf.at[zh, y, zl, core], loc.at[1])
    own_w.start()

    def ay_copy(k):
        seq, head = at_yz(lax.rem(y + k, 4), z, core)
        return remote(
            wt_ref.at[:, LO], wbuf.at[zh, y, zl, core, :, LO], ays.at[k], ayr.at[k], seq, head
        )

    def ay_wait(k):
        yf = lax.rem(y + 4 - k, 4)
        return remote(
            wt_ref.at[:, LO], wbuf.at[zh, yf, zl, core, :, LO], ays.at[k], ayr.at[k], s, h
        )

    def z_set(o, colour):
        if colour == 0:
            return wbuf.at[o // 4, :, lax.rem(o, 4), core, :, LO]
        return wbuf.at[o // 4, y, lax.rem(o, 4), core, :, HI]

    def zp_copy(k, colour, wait):
        o = lax.rem(z - k + 8 + (0 if wait else 1), 8)
        ss, rs = (azps, azpr) if colour == 0 else (bzps, bzpr)
        seq, head = at_yz(y, lax.rem(z + 1, 8), core)
        return remote(z_set(o, colour), z_set(o, colour), ss.at[k], rs.at[k], seq, head)

    def zm_copy(k, colour, wait):
        o = lax.rem(z + k - (0 if wait else 1), 8)
        ss, rs = (azms, azmr) if colour == 0 else (bzms, bzmr)
        seq, head = at_yz(y, lax.rem(z + 7, 8), core)
        return remote(z_set(o, colour), z_set(o, colour), ss.at[k], rs.at[k], seq, head)

    def by_set(y_):
        return wbuf.at[:, y_, :, core, :, HI]

    def by_copy(k):
        seq, head = at_yz(lax.rem(y + k, 4), z, core)
        return remote(by_set(y), by_set(y), bys.at[k], byr.at[k], seq, head)

    def by_wait(k):
        yf = lax.rem(y + 4 - k, 4)
        return remote(by_set(yf), by_set(yf), bys.at[k], byr.at[k], s, h)

    def fa_copy(o, c_):
        ref = wbuf.at[o // 4, :, lax.rem(o, 4), c_, :, LO]
        return remote(ref, ref, fas.at[o], far.at[o], sib, h)

    def fb_copy(y_, c_):
        ref = wbuf.at[:, y_, :, c_, :, HI]
        return remote(ref, ref, fbs.at[y_], fbr.at[y_], sib, h)

    for k in range(1, 4):
        ay_copy(k).start()
    seq_p, head_p = at_yz(y, lax.rem(z + 1, 8), core)
    seq_m, head_m = at_yz(y, lax.rem(z + 7, 8), core)
    bz_first_p = remote(
        wt_ref.at[:, HI], wbuf.at[zh, y, zl, core, :, HI], bzps.at[1], bzpr.at[1], seq_p, head_p
    )
    bz_first_m = remote(
        wt_ref.at[:, HI], wbuf.at[zh, y, zl, core, :, HI], bzms.at[1], bzmr.at[1], seq_m, head_m
    )
    bz_first_p.start()
    bz_first_m.start()

    def w_step(n):
        if n == 1:
            own_w.wait()
            for k in range(1, 4):
                ay_wait(k).wait_recv()
            zp_copy(1, 0, False).start()
            zm_copy(1, 0, False).start()
            fa_copy(z, core).start()
            zp_copy(1, 1, True).wait_recv()
            zp_copy(2, 1, False).start()
            zm_copy(1, 1, True).wait_recv()
            zm_copy(2, 1, False).start()
        if n == 2:
            zp_copy(1, 0, True).wait_recv()
            zp_copy(2, 0, False).start()
            zm_copy(1, 0, True).wait_recv()
            zm_copy(2, 0, False).start()
            fa_copy(lax.rem(z + 7, 8), core).start()
            fa_copy(lax.rem(z + 1, 8), core).start()
            zp_copy(2, 1, True).wait_recv()
            zp_copy(3, 1, False).start()
            zm_copy(2, 1, True).wait_recv()
            zm_copy(3, 1, False).start()
        if n == 3:
            zp_copy(3, 1, True).wait_recv()
            zp_copy(4, 1, False).start()
            zm_copy(3, 1, True).wait_recv()
            zp_copy(2, 0, True).wait_recv()
            zp_copy(3, 0, False).start()
            zm_copy(2, 0, True).wait_recv()
            zm_copy(3, 0, False).start()
            fa_copy(lax.rem(z + 6, 8), core).start()
            fa_copy(lax.rem(z + 2, 8), core).start()
        if n == 4:
            zp_copy(4, 1, True).wait_recv()
            for k in range(1, 4):
                by_copy(k).start()
            fb_copy(y, core).start()
        if n == 5:
            zp_copy(3, 0, True).wait_recv()
            zp_copy(4, 0, False).start()
            zm_copy(3, 0, True).wait_recv()
            fa_copy(lax.rem(z + 5, 8), core).start()
            fa_copy(lax.rem(z + 3, 8), core).start()
        if n == 6:
            zp_copy(4, 0, True).wait_recv()
            fa_copy(lax.rem(z + 4, 8), core).start()
            for k in range(1, 4):
                by_wait(k).wait_recv()
                fb_copy(lax.rem(y + 4 - k, 4), core).start()
        if n == 7:
            for o in range(8):
                fa_copy(o, 1 - core).wait_recv()
            for y_ in range(4):
                fb_copy(y_, 1 - core).wait_recv()

    kvbuf[0] = kv_ref[...]
    docbuf[0] = doc_ref[...]
    docq[core] = doc_ref[...]
    own_rows = pl.ds(core * ROWS, ROWS)
    for g in range(GROUP):
        q8[g, own_rows, :] = q_ref[:, g * HD:(g + 1) * HD]
        go8[g, own_rows, :] = go_ref[:, g * HD:(g + 1) * HD]
    for j in range(SPAN):
        mxb[j] = jnp.full((8, 2048), FLOOR, jnp.float32)
        lsb[j] = jnp.zeros((8, 2048), jnp.float32)
        dsb[j] = jnp.zeros((8, 2048), jnp.float32)

        @pl.when(chip < j)
        def _():
            kvbuf[j] = jnp.zeros((ROWS, 256), jnp.bfloat16)
            dsbuf[j] = jnp.zeros((ROWS, 2048), jnp.bfloat16)

    docq_wait.wait_recv()
    for g in range(GROUP):
        q_wait(g).wait_recv()
        go_wait(g).wait_recv()

    def forward(j, _):
        @pl.when(chip >= j)
        def _():
            @pl.when(j > 0)
            def _():
                doc_copy(j).wait_recv()
                kv_copy(j).wait_recv()

            ids = docbuf[j]
            drow = jnp.concatenate((docq[0], docq[1]), axis=1)
            low = jnp.zeros((1, 256), jnp.float32)
            for v in range(3):
                count = jnp.sum((ids == v).astype(jnp.float32), axis=1, keepdims=True)
                low = low + jnp.where(drow > v, count, 0.0)
            place = lax.broadcasted_iota(jnp.int32, (ROWS, 256), 0)
            token = lax.broadcasted_iota(jnp.int32, (ROWS, 256), 1)
            high = jnp.where(j == 0, token - core * ROWS, ROWS)
            keep = (place >= low.astype(jnp.int32)) & (place <= high)
            bias[...] = jnp.where(keep, 0.0, NEG)
            key_rows = kvbuf[j, :, :HD]
            value_rows = kvbuf[j, :, HD:]
            for g in range(GROUP):
                cols = slice(g * 256, (g + 1) * 256)
                logits = lax.dot_general(
                    key_rows, q8[g], NT, preferred_element_type=jnp.float32
                )
                grad_p = lax.dot_general(
                    value_rows, go8[g], NT, preferred_element_type=jnp.float32
                )
                logits = logits + bias[...]
                top = jnp.maximum(jnp.max(logits, axis=0, keepdims=True), FLOOR)
                weight = jnp.exp2((logits - top) * EXP_SCALE)
                ebuf[j, :, cols] = weight
                dpbuf[j, :, cols] = grad_p
                mxb[j, :, cols] = jnp.broadcast_to(top, (8, 256))
                lsb[j, :, cols] = jnp.sum(weight.reshape(16, 8, 256), axis=0)
                dsb[j, :, cols] = jnp.sum((weight * grad_p).reshape(16, 8, 256), axis=0)

        @pl.when(j == 4)
        def _():
            w_step(1)

        return 0

    lax.fori_loop(0, SPAN, forward, 0)
    w_step(2)

    top = mxb[0]
    for j in range(1, SPAN):
        top = jnp.maximum(top, mxb[j])
    total = jnp.zeros((8, 2048), jnp.float32)
    dots = jnp.zeros((8, 2048), jnp.float32)
    for j in range(SPAN):
        factor = jnp.exp2((mxb[j] - top) * EXP_SCALE)
        total = total + factor * lsb[j]
        dots = dots + factor * dsb[j]
    total = jnp.sum(total, axis=0, keepdims=True)
    dots = jnp.sum(dots, axis=0, keepdims=True)
    row = lax.broadcasted_iota(jnp.int32, (8, 2048), 0)
    stat[...] = jnp.where(row == 0, top, jnp.where(row == 1, total, dots))
    stat_copy = remote(stat, strecv, sts, str_, sib, h)
    stat_copy.start()
    stat_copy.wait_recv()
    m_own, m_far = stat[0:1], strecv[0:1]
    m_all = jnp.maximum(m_own, m_far)
    f_own = jnp.exp2((m_own - m_all) * EXP_SCALE)
    f_far = jnp.exp2((m_far - m_all) * EXP_SCALE)
    l_all = stat[1:2] * f_own + strecv[1:2] * f_far
    d_all = (stat[2:3] * f_own + strecv[2:3] * f_far) / l_all
    stat_copy.wait_send()
    stat[0:1] = m_all
    stat[1:2] = 1.0 / l_all
    stat[2:3] = d_all

    def dk_copy(j):
        return remote(
            sendbuf.at[j], dkvrecv.at[j], dks.at[j], dkr.at[j], lax.rem(s - 2 * j + 32, 32), h
        )

    def backward(i, _):
        j = SPAN - 1 - i

        @pl.when(chip >= j)
        def _():
            for g in range(GROUP):
                cols = slice(g * 256, (g + 1) * 256)
                factor = jnp.exp2((mxb[j, 0:1, cols] - stat[0:1, cols]) * EXP_SCALE)
                factor = factor * stat[1:2, cols]
                probs = ebuf[j, :, cols] * factor
                pbuf[:, cols] = probs.astype(jnp.bfloat16)
                grad_l = probs * (dpbuf[j, :, cols] - stat[2:3, cols])
                dsbuf[j, :, cols] = grad_l.astype(jnp.bfloat16)
            grad_k = jnp.dot(
                dsbuf[j], q8[...].reshape(2048, HD), preferred_element_type=jnp.float32
            )
            grad_v = jnp.dot(
                pbuf[...], go8[...].reshape(2048, HD), preferred_element_type=jnp.float32
            )
            grad_k = grad_k * SCALE
            ownbuf[:, :HD] = grad_k
            ownbuf[:, HD:] = grad_v

            @pl.when(j > 0)
            def _():
                sendbuf[j, :, :HD] = grad_k.astype(jnp.bfloat16)
                sendbuf[j, :, HD:] = grad_v.astype(jnp.bfloat16)
                dk_copy(j).start()

        @pl.when(i == 4)
        def _():
            w_step(3)

        return 0

    lax.fori_loop(0, SPAN, backward, 0)
    w_step(4)

    key_t = jnp.concatenate([jnp.transpose(kvbuf[j, :, :HD]) for j in range(SPAN)], axis=1)
    for g in range(GROUP):
        grad_t = jnp.dot(
            key_t,
            dsbuf[:, :, g * 256:(g + 1) * 256].reshape(SPAN * ROWS, 256),
            preferred_element_type=jnp.float32,
        )
        dqbuf[:, g * HD:(g + 1) * HD] = jnp.transpose(grad_t) * SCALE
    dq_copy = remote(dqbuf.at[pl.ds((1 - core) * ROWS, ROWS)], dqrecv, dqs, dqr, sib, h)
    dq_copy.start()
    w_step(5)

    acc = ownbuf[...]
    ownbuf[...] = acc
    for j in range(1, SPAN):

        @pl.when(chip + j <= 15)
        def _():
            dk_copy(j).wait_recv()
            ownbuf[...] += dkvrecv[j].astype(jnp.float32)

    grad_kv = ownbuf[...].astype(jnp.bfloat16)
    gkv_ref[...] = grad_kv
    gbuf[h] = grad_kv

    z_send = remote(gbuf.at[h], gbuf.at[h], g1s, g1r, s, x * 2 + 1 - zh)
    z_wait = remote(gbuf.at[h], gbuf.at[x * 2 + 1 - zh], g1s, g1r, s, x * 2 + 1 - zh)
    z_send.start()

    def gx_copy(k, far):
        hh = (x * 2 + 1 - zh) if far else h
        xt = lax.rem(x + k, 4)
        n = k + (4 if far else 0)
        return remote(gbuf.at[hh], gbuf.at[hh], gxs.at[n], gxr.at[n], s, xt * 2 + zh)

    def gx_wait(k, far):
        xf = lax.rem(x + 4 - k, 4)
        hh = xf * 2 + ((1 - zh) if far else zh)
        n = k + (4 if far else 0)
        return remote(gbuf.at[hh], gbuf.at[hh], gxs.at[n], gxr.at[n], s, h)

    for k in range(1, 4):
        gx_copy(k, False).start()
    dq_copy.wait_recv()
    gq_ref[...] = (dqbuf[own_rows, :] + dqrecv[...]).astype(jnp.bfloat16)
    z_wait.wait_recv()
    for k in range(1, 4):
        gx_copy(k, True).start()

    w_step(6)
    own_delta.wait()
    for k in range(1, 4):
        del_wait(k).wait_recv()
    w_step(7)

    def project(n, _):
        out = None
        for b in range(2):
            left = dbuf[:, :, b * 1024:(b + 1) * 1024].reshape(512, 1024)
            right = wbuf[b, n].reshape(512, 1024)
            part = lax.dot_general(left, right, NT, preferred_element_type=jnp.float32)
            out = part if out is None else out + part
        pbig[n] = out
        return 0

    lax.fori_loop(0, 4, project, 0)
    for k in range(1, 4):
        gx_wait(k, False).wait_recv()
        gx_wait(k, True).wait_recv()

    lane = lax.broadcasted_iota(jnp.int32, (8, 128), 1)
    sub = lax.broadcasted_iota(jnp.int32, (8, 128), 0)
    tile = jnp.zeros((8, 128), jnp.float32)
    for hh in range(8):
        grads = gbuf[hh].astype(jnp.float32)
        off = (hh % 2) * 256
        for i in range(4):
            prod = pbig[hh // 2, i * 128:(i + 1) * 128, off:off + 256] * grads
            prod = jnp.sum(prod.reshape(16, 8, 256), axis=0)
            prod = jnp.sum(prod, axis=0, keepdims=True)
            for n in range(2):
                value = jnp.sum(prod[:, n * 128:(n + 1) * 128], axis=1, keepdims=True)
                hit = (sub == 2 * i + zh) & (lane == 2 * hh + n)
                tile = jnp.where(hit, value, tile)
    tile = tile * (1.0 / 64.0)

    def reduce_over(tile, n, me, peer, buf, src, ss, rs):
        src[...] = tile
        buf[me] = tile
        for k in range(1, n):
            to = lax.rem(me + k, n)
            seq, head = peer(to)
            remote(src, buf.at[me], ss.at[k], rs.at[k], seq, head).start()
        for k in range(1, n):
            frm = lax.rem(me + n - k, n)
            remote(src, buf.at[frm], ss.at[k], rs.at[k], s, h).wait_recv()
        out = buf[0]
        for k in range(1, n):
            out = out + buf[k]
        return out

    tile = reduce_over(
        tile, 8, y * 2 + core, lambda t: at_yz(t // 2, z, lax.rem(t, 2)), ar1, arsrc.at[0], a1s, a1r
    )
    tile = reduce_over(tile, 8, z, lambda t: at_yz(y, t, core), ar2, arsrc.at[1], a2s, a2r)
    tile = reduce_over(tile, 4, x, lambda t: (s, t * 2 + zh), ar3, arsrc.at[2], a3s, a3r)
    sc_ref[...] = tile

    docq_send.wait_send()
    for g in range(GROUP):
        q_copy(g).wait_send()
        go_copy(g).wait_send()
    for j in range(1, SPAN):

        @pl.when(chip + j <= 15)
        def _():
            doc_copy(j).wait_send()
            kv_copy(j).wait_send()

        @pl.when(chip >= j)
        def _():
            dk_copy(j).wait_send()

    for k in range(1, 4):
        del_copy(k).wait_send()
        ay_copy(k).wait_send()
        by_copy(k).wait_send()
        gx_copy(k, False).wait_send()
        gx_copy(k, True).wait_send()
    for k in range(1, 5):
        for colour in range(2):
            zp_copy(k, colour, False).wait_send()
            if k < 4:
                zm_copy(k, colour, False).wait_send()
    for o in range(8):
        fa_copy(o, core).wait_send()
    for y_ in range(4):
        fb_copy(y_, core).wait_send()
    dq_copy.wait_send()
    z_send.wait_send()
    for n, src, buf, ss, rs in (
        (8, arsrc.at[0], ar1, a1s, a1r),
        (8, arsrc.at[1], ar2, a2s, a2r),
        (4, arsrc.at[2], ar3, a3s, a3r),
    ):
        for k in range(1, n):
            remote(src, buf.at[0], ss.at[k], rs.at[k], s, h).wait_send()


def on_device(queries, keyval, grad_out, doc_ids, deltas, node_weights, layer_slot):
    vmem = pl.BlockSpec(memory_space=pltpu.VMEM)
    hbm = pl.BlockSpec(memory_space=pl.ANY)
    bf, f32, i32 = jnp.bfloat16, jnp.float32, jnp.int32
    V, D = pltpu.VMEM, pltpu.SemaphoreType.DMA
    scratch = [
        V((8, 256, 128), bf),
        V((8, 256, 128), bf),
        V((SPAN, 128, 256), bf),
        V((SPAN, 1, 128), i32),
        V((2, 1, 128), i32),
        V((128, 256), f32),
        V((SPAN, 128, 2048), f32),
        V((SPAN, 128, 2048), f32),
        V((SPAN, 8, 2048), f32),
        V((SPAN, 8, 2048), f32),
        V((SPAN, 8, 2048), f32),
        V((8, 2048), f32),
        V((8, 2048), f32),
        V((128, 2048), bf),
        V((SPAN, 128, 2048), bf),
        V((SPAN, 128, 256), bf),
        V((SPAN, 128, 256), bf),
        V((128, 256), f32),
        V((256, 1024), f32),
        V((128, 1024), f32),
        V((4, 128, 2048), bf),
        V((2, 4, 4, 2, 64, 1024), bf),
        V((4, 512, 512), f32),
        V((8, 128, 256), bf),
        V((3, 8, 128), f32),
        V((8, 8, 128), f32),
        V((8, 8, 128), f32),
        V((4, 8, 128), f32),
    ]
    sems = [
        9, 9, 9, 9, 16, 16, None, None, 9, 9, None, None, 4, 4, 2,
        4, 4, 5, 5, 4, 4, 5, 5, 4, 4, 4, 4, 8, 8, 4, 4, None, None, 8, 8,
        8, 8, 8, 8, 4, 4,
    ]
    scratch += [D if n is None else D((n,)) for n in sems]
    grad_query, grad_keyval, tile = pl.pallas_call(
        kernel,
        out_shape=(
            jax.ShapeDtypeStruct((128, 1024), bf),
            jax.ShapeDtypeStruct((128, 256), bf),
            jax.ShapeDtypeStruct((8, 128), f32),
        ),
        in_specs=[vmem, vmem, vmem, vmem, hbm, vmem],
        out_specs=(vmem, vmem, vmem),
        scratch_shapes=scratch,
        compiler_params=pltpu.CompilerParams(
            has_side_effects=True, vmem_limit_bytes=60 * 1024 * 1024
        ),
    )(
        queries,
        keyval,
        grad_out,
        doc_ids.reshape(1, 128),
        deltas.reshape(128, 8192),
        node_weights.T,
    )
    placing = (layer_slot[:, None] == jnp.arange(8, dtype=jnp.int32)[None, :]).astype(f32)
    scores = jnp.dot(placing.T, tile[:, :16], precision=lax.Precision.HIGHEST)
    return (grad_query, grad_keyval, scores)


def solution(mesh):
    return jax.shard_map(
        on_device,
        mesh=mesh,
        in_specs=(
            P("seq", "head"),
            P("seq", "head"),
            P("seq", "head"),
            P("seq"),
            P("head", "seq", None),
            P("head", "seq"),
            P(),
        ),
        out_specs=(P("seq", "head"), P("seq", "head"), P()),
        check_vma=False,
    )
```

time: 493 us -> 107 us (0.22)
  blocking collectives: 220 us -> 0 us
  Pallas kernels: 0 us -> 101 us
  waiting for transfers between devices: 74.2 us -> 0 us
  matrix products: 70.4 us -> 1.52 us
  other arithmetic: 56.2 us -> 0 us
  local copies, waits for them, and re-layouts: 53.7 us -> 3.14 us
  between operations: 13.9 us -> 0.66 us
    pallas_call x0 -> x1, Pallas kernels: none -> 101 us  [on_device(): pl.pallas_call(kernel, out_shape=(jax.ShapeDtypeStruct((128, 1024), bf),...]
    all_gather x2 -> x0, blocking collectives: 85.5 us -> none  [the longest x1 47.9 us: on_device(): grad_rows = lax.all_gather(grad_keyval, 'head', axis=1, tiled=True)]
    psum x1 -> x0, blocking collectives: 76.2 us -> none  [on_device(): totals = lax.psum(partial_value / math.sqrt(seq_total), ('seq', 'head'))]
    dot_general x58 -> x1, matrix products: 70.4 us -> 1.52 us  [on_device(): scores = jnp.dot(placing.T, tile[:, :16], precision=lax.Precision.HIGHEST)]
    all_to_all x1 -> x0, blocking collectives: 58.4 us -> none  [on_device(): lax.all_to_all(deltas, 'head', split_axis=2, concat_axis=0, tiled=True)]
    all_gather x2 -> x0, waiting for transfers between devices: 56.2 us -> none  [the longest x1 31 us: on_device(): lax.all_gather(node_weights, 'seq', axis=1, tiled=True)]
    unnamed x6 -> x0, other arithmetic: 46.5 us -> none
    unnamed x19 -> x4, local copies, waits for them, and re-layouts: 25.4 us -> 3.14 us
  transfers between devices with their start and end apart: 3 -> 0, of which waited for: 3 -> 0; matrix products, arithmetic and copies ran while one was open for 15% -> 0% of each run, Pallas kernels for 0% -> 0%
where the time goes in v1:
time: 107 us
  Pallas kernels  101 us (94%)
  local copies, waits for them, and re-layouts  3.14 us (3%)
  matrix products  1.52 us (1%)
    pallas_call x1, Pallas kernels, on_device(): pl.pallas_call(kernel, out_shape=(jax.ShapeDtypeStruct((128, 1024), bf),...  101 us
    unnamed x4, local copies, waits for them, and re-layouts  3.14 us

profile of v1, /device:TPU:8, one launch (start us, length us, event | category | flops | bytes accessed | tf_op | source)
XLA Modules:
  0.0 106.6 jit_solution(4813834742146487305)
XLA Ops:
  0.6 0.0 copy-start
  0.6 101.3 %shard_map.94 = (bf16[128,1024]{1,0:T(8,128)(2,1)}, bf16[128,256]{1,0:T(8,128)(2,1)}, f32[8,128]{1,0:T(8,128)}) custom-call(bf16[128,1024]{1,0:T(8,128)(2,1)} %q_ref.1, bf16[128,256]{1,0:T(8,128)(2,1)} %kv_ref.1, bf16[128,1024]{1,0:T(8,128)(2,1)} %go_ref.1, s32[1,128]{1,0:T(1,128)} %bitcast.5, bf16[128,8192]{1,0:T(8,128)(2,1)} %bitcast.3, ...), custom_call_target="tpu_custom_call" | custom-call | tf_op jit(solution)/shard_map/pallas_call | solution.py:665
  102.0 0.0 copy-done
  102.0 1.5 %fusion = f32[8,16]{1,0:T(8,128)} fusion(f32[8,128]{1,0:T(8,128)} %get-tuple-element.8, s32[8]{0:T(128)S(1)} %copy-done), kind=kOutput, calls=%fused_computation | convolution fusion | flops 12352 | bytes 4640 | tf_op jit(solution)/shard_map/dot_general | solution.py:687
  103.5 1.7 %copy.12 = bf16[128,1024]{1,0:T(8,128)(2,1)} copy(bf16[128,1024]{1,0:T(8,128)(2,1)} %get-tuple-element.12) | data formatting | bytes 524288
  105.2 1.5 %copy.13 = bf16[128,256]{1,0:T(8,128)(2,1)} copy(bf16[128,256]{1,0:T(8,128)(2,1)} %get-tuple-element.13) | data formatting | bytes 131072
Async XLA Ops:
  0.6 101.3 %copy-start = (s32[8]{0:T(128)S(1)}, s32[8]{0:T(128)}, u32[]{:S(2)}) copy-start(s32[8]{0:T(128)} %param.13) | copy-start | bytes 100

commit v2 on v1

--- a/solution.py
+++ b/solution.py
@@ -11,6 +11,7 @@
 GROUP = 8
 ROWS = 128
 SPAN = 9
+CUT = 384
 NEG = -1e30
 FLOOR = -1e29
 SCALE = 1.0 / math.sqrt(HD)
@@ -85,20 +86,16 @@
     loc,
     ays,
     ayr,
-    azps,
-    azpr,
-    azms,
-    azmr,
-    bzps,
-    bzpr,
-    bzms,
-    bzmr,
+    azs,
+    azr,
+    bzs,
+    bzr,
     bys,
     byr,
-    fas,
-    far,
-    fbs,
-    fbr,
+    bos,
+    bor,
+    fs,
+    fr,
     g1s,
     g1r,
     gxs,
@@ -170,18 +167,33 @@
             h,
         )
 
+    barrier = pltpu.get_barrier_semaphore()
+
+    def greet(seq, head):
+        pl.semaphore_signal(barrier, inc=1, device_id=(seq, head), device_id_type=MESH)
+
+    for k in range(1, 16):
+        greet(lax.rem(s + 2 * k, 32), h)
+    for k in range(4):
+        greet(lax.rem(y + k, 4) * 8 + zl * 2 + 1 - core, h)
+        greet(y * 8 + k * 2 + core, x * 2 + 1 - zh)
+    for k in range(1, 4):
+        greet(s, lax.rem(x + k, 4) * 2 + zh)
+    pl.semaphore_wait(barrier, 26)
+
     docq_send = remote(doc_ref, docq.at[core], docs.at[0], docr.at[0], sib, h)
     docq_wait = remote(doc_ref, docq.at[1 - core], docs.at[0], docr.at[0], sib, h)
     docq_send.start()
+    for j in range(1, SPAN):
+
+        @pl.when(chip + j <= 15)
+        def _():
+            doc_copy(j).start()
+            kv_copy(j).start()
+
     for g in range(GROUP):
         q_copy(g).start()
         go_copy(g).start()
-    for j in range(1, SPAN):
-
-        @pl.when(chip + j <= 15)
-        def _():
-            doc_copy(j).start()
-            kv_copy(j).start()
 
     def del_copy(k):
         xt = lax.rem(x + k, 4)
@@ -212,126 +224,143 @@
     )
     own_delta.start()
 
-    LO, HI = pl.ds(0, 512), pl.ds(512, 512)
+    LA, LB = pl.ds(0, CUT), pl.ds(CUT, 1024 - CUT)
+    sent = {}
+
+    def send(build, *args):
+        build(*args).start()
+        sent[(build, args)] = True
+
+    def piece(r, m, lanes, c_=None):
+        o = lax.rem(z + r, 8)
+        return wbuf.at[
+            o // 4, lax.rem(y + 4 - m, 4), lax.rem(o, 4), core if c_ is None else c_, :, lanes
+        ]
+
+    def to_y(k):
+        return at_yz(lax.rem(y + k, 4), z, core)
+
+    def to_z(d):
+        return at_yz(y, lax.rem(z + d + 8, 8), core)
+
+    def ay(k, wait=False):
+        dst = piece(0, k if wait else 0, LA)
+        return remote(wt_ref.at[:, LA], dst, ays.at[k], ayr.at[k], *to_y(k))
+
+    def az(d, k, m, wait=False):
+        ref = piece((-d * (k if wait else k - 1)) % 8, m, LA)
+        src = wt_ref.at[:, LA] if (k == 1 and m == 0) else ref
+        n = ((d < 0) * 5 + k) * 4 + m
+        return remote(src, ref, azs.at[n], azr.at[n], *to_z(d))
+
+    def bz(d, k, wait=False):
+        ref = piece((-d * (k if wait else k - 1)) % 8, 0, LB)
+        src = wt_ref.at[:, LB] if k == 1 else ref
+        n = (d < 0) * 5 + k
+        return remote(src, ref, bzs.at[n], bzr.at[n], *to_z(d))
+
+    def by(d, r, wait=False):
+        ref = piece(r, (d % 4) if wait else 0, LB)
+        src = wt_ref.at[:, LB] if r == 0 else ref
+        n = (d < 0) * 8 + r
+        return remote(src, ref, bys.at[n], byr.at[n], *to_y(d % 4))
+
+    def bo(d, r, wait=False):
+        ref = piece(r, 2 if wait else d % 4, LB)
+        return remote(ref, ref, bos.at[r], bor.at[r], *to_y(d % 4))
+
+    def own_row():
+        ref = wbuf.at[zh, y, zl, core]
+        return remote(wt_ref, ref, fs.at[0], fr, sib, h)
+
+    def fa(r, m):
+        ref = piece(r, m, LA)
+        return remote(ref, ref, fs.at[r * 4 + m], fr, sib, h)
+
+    def fb(r, m):
+        ref = piece(r, m, LB)
+        return remote(ref, ref, fs.at[32 + r * 4 + m], fr, sib, h)
+
     own_w = pltpu.make_async_copy(wt_ref, wbuf.at[zh, y, zl, core], loc.at[1])
     own_w.start()
-
-    def ay_copy(k):
-        seq, head = at_yz(lax.rem(y + k, 4), z, core)
-        return remote(
-            wt_ref.at[:, LO], wbuf.at[zh, y, zl, core, :, LO], ays.at[k], ayr.at[k], seq, head
-        )
-
-    def ay_wait(k):
-        yf = lax.rem(y + 4 - k, 4)
-        return remote(
-            wt_ref.at[:, LO], wbuf.at[zh, yf, zl, core, :, LO], ays.at[k], ayr.at[k], s, h
-        )
-
-    def z_set(o, colour):
-        if colour == 0:
-            return wbuf.at[o // 4, :, lax.rem(o, 4), core, :, LO]
-        return wbuf.at[o // 4, y, lax.rem(o, 4), core, :, HI]
-
-    def zp_copy(k, colour, wait):
-        o = lax.rem(z - k + 8 + (0 if wait else 1), 8)
-        ss, rs = (azps, azpr) if colour == 0 else (bzps, bzpr)
-        seq, head = at_yz(y, lax.rem(z + 1, 8), core)
-        return remote(z_set(o, colour), z_set(o, colour), ss.at[k], rs.at[k], seq, head)
-
-    def zm_copy(k, colour, wait):
-        o = lax.rem(z + k - (0 if wait else 1), 8)
-        ss, rs = (azms, azmr) if colour == 0 else (bzms, bzmr)
-        seq, head = at_yz(y, lax.rem(z + 7, 8), core)
-        return remote(z_set(o, colour), z_set(o, colour), ss.at[k], rs.at[k], seq, head)
-
-    def by_set(y_):
-        return wbuf.at[:, y_, :, core, :, HI]
-
-    def by_copy(k):
-        seq, head = at_yz(lax.rem(y + k, 4), z, core)
-        return remote(by_set(y), by_set(y), bys.at[k], byr.at[k], seq, head)
-
-    def by_wait(k):
-        yf = lax.rem(y + 4 - k, 4)
-        return remote(by_set(yf), by_set(yf), bys.at[k], byr.at[k], s, h)
-
-    def fa_copy(o, c_):
-        ref = wbuf.at[o // 4, :, lax.rem(o, 4), c_, :, LO]
-        return remote(ref, ref, fas.at[o], far.at[o], sib, h)
-
-    def fb_copy(y_, c_):
-        ref = wbuf.at[:, y_, :, c_, :, HI]
-        return remote(ref, ref, fbs.at[y_], fbr.at[y_], sib, h)
-
-    for k in range(1, 4):
-        ay_copy(k).start()
-    seq_p, head_p = at_yz(y, lax.rem(z + 1, 8), core)
-    seq_m, head_m = at_yz(y, lax.rem(z + 7, 8), core)
-    bz_first_p = remote(
-        wt_ref.at[:, HI], wbuf.at[zh, y, zl, core, :, HI], bzps.at[1], bzpr.at[1], seq_p, head_p
-    )
-    bz_first_m = remote(
-        wt_ref.at[:, HI], wbuf.at[zh, y, zl, core, :, HI], bzms.at[1], bzmr.at[1], seq_m, head_m
-    )
-    bz_first_p.start()
-    bz_first_m.start()
+    for d in (1, -1):
+        send(bz, d, 1)
+    for k in (1, 3, 2):
+        send(ay, k)
+    for d in (1, -1):
+        send(az, d, 1, 0)
+        send(by, d, 0)
+    send(own_row)
+    STEPS = {1: 4, -1: 3}
+
+    def a_ring(k, ms):
+        for m in ms:
+            for d in (1, -1):
+                if k <= STEPS[d]:
+                    az(d, k, m, True).wait_recv()
+                    if k < STEPS[d]:
+                        send(az, d, k + 1, m)
+                    send(fa, (-d * k) % 8, m)
+
+    def b_ring(k):
+        for d in (1, -1):
+            if k <= STEPS[d]:
+                bz(d, k, True).wait_recv()
+                if k < STEPS[d]:
+                    send(bz, d, k + 1)
+                r = (-d * k) % 8
+                send(by, 1, r)
+                send(by, -1, r)
+                send(fb, r, 0)
+
+    def b_side(k):
+        for r in sorted({k, -k % 8}):
+            for d in (1, -1):
+                by(d, r, True).wait_recv()
+                if (d > 0) == (r < 4):
+                    send(bo, d, r)
+                send(fb, r, d % 4)
+
+    def b_far(k):
+        for r in sorted({k, -k % 8}):
+            bo(1 if r < 4 else -1, r, True).wait_recv()
+            send(fb, r, 2)
 
     def w_step(n):
         if n == 1:
+            b_ring(1)
+            for k in (1, 3, 2):
+                ay(k, True).wait_recv()
+                send(az, 1, 1, k)
+                send(az, -1, 1, k)
+                send(fa, 0, k)
+            a_ring(1, (0,))
+            b_side(0)
+        if n == 2:
+            b_ring(2)
+            a_ring(1, (1, 3, 2))
+            b_side(1)
+            b_far(0)
+        if n == 3:
+            b_ring(3)
+            a_ring(2, (0, 1, 3, 2))
+            b_side(2)
+            b_far(1)
+        if n == 4:
+            b_ring(4)
+            a_ring(3, (0, 1, 3, 2))
+            b_side(3)
+            b_far(2)
+        if n == 5:
+            a_ring(4, (0, 1, 3, 2))
+            b_side(4)
+            b_far(3)
+        if n == 6:
+            b_far(4)
+        if n == 7:
             own_w.wait()
-            for k in range(1, 4):
-                ay_wait(k).wait_recv()
-            zp_copy(1, 0, False).start()
-            zm_copy(1, 0, False).start()
-            fa_copy(z, core).start()
-            zp_copy(1, 1, True).wait_recv()
-            zp_copy(2, 1, False).start()
-            zm_copy(1, 1, True).wait_recv()
-            zm_copy(2, 1, False).start()
-        if n == 2:
-            zp_copy(1, 0, True).wait_recv()
-            zp_copy(2, 0, False).start()
-            zm_copy(1, 0, True).wait_recv()
-            zm_copy(2, 0, False).start()
-            fa_copy(lax.rem(z + 7, 8), core).start()
-            fa_copy(lax.rem(z + 1, 8), core).start()
-            zp_copy(2, 1, True).wait_recv()
-            zp_copy(3, 1, False).start()
-            zm_copy(2, 1, True).wait_recv()
-            zm_copy(3, 1, False).start()
-        if n == 3:
-            zp_copy(3, 1, True).wait_recv()
-            zp_copy(4, 1, False).start()
-            zm_copy(3, 1, True).wait_recv()
-            zp_copy(2, 0, True).wait_recv()
-            zp_copy(3, 0, False).start()
-            zm_copy(2, 0, True).wait_recv()
-            zm_copy(3, 0, False).start()
-            fa_copy(lax.rem(z + 6, 8), core).start()
-            fa_copy(lax.rem(z + 2, 8), core).start()
-        if n == 4:
-            zp_copy(4, 1, True).wait_recv()
-            for k in range(1, 4):
-                by_copy(k).start()
-            fb_copy(y, core).start()
-        if n == 5:
-            zp_copy(3, 0, True).wait_recv()
-            zp_copy(4, 0, False).start()
-            zm_copy(3, 0, True).wait_recv()
-            fa_copy(lax.rem(z + 5, 8), core).start()
-            fa_copy(lax.rem(z + 3, 8), core).start()
-        if n == 6:
-            zp_copy(4, 0, True).wait_recv()
-            fa_copy(lax.rem(z + 4, 8), core).start()
-            for k in range(1, 4):
-                by_wait(k).wait_recv()
-                fb_copy(lax.rem(y + 4 - k, 4), core).start()
-        if n == 7:
-            for o in range(8):
-                fa_copy(o, 1 - core).wait_recv()
-            for y_ in range(4):
-                fb_copy(y_, 1 - core).wait_recv()
+            far = wbuf.at[:, :, :, 1 - core]
+            remote(far, far, fs.at[0], fr, sib, h).wait_recv()
 
     kvbuf[0] = kv_ref[...]
     docbuf[0] = doc_ref[...]
@@ -341,12 +370,12 @@
         q8[g, own_rows, :] = q_ref[:, g * HD:(g + 1) * HD]
         go8[g, own_rows, :] = go_ref[:, g * HD:(g + 1) * HD]
     for j in range(SPAN):
-        mxb[j] = jnp.full((8, 2048), FLOOR, jnp.float32)
-        lsb[j] = jnp.zeros((8, 2048), jnp.float32)
-        dsb[j] = jnp.zeros((8, 2048), jnp.float32)
 
         @pl.when(chip < j)
         def _():
+            mxb[j] = jnp.full((8, 2048), FLOOR, jnp.float32)
+            lsb[j] = jnp.zeros((8, 2048), jnp.float32)
+            dsb[j] = jnp.zeros((8, 2048), jnp.float32)
             kvbuf[j] = jnp.zeros((ROWS, 256), jnp.bfloat16)
             dsbuf[j] = jnp.zeros((ROWS, 2048), jnp.bfloat16)
 
@@ -393,14 +422,13 @@
                 lsb[j, :, cols] = jnp.sum(weight.reshape(16, 8, 256), axis=0)
                 dsb[j, :, cols] = jnp.sum((weight * grad_p).reshape(16, 8, 256), axis=0)
 
-        @pl.when(j == 4)
+        @pl.when(j == 5)
         def _():
             w_step(1)
 
         return 0
 
     lax.fori_loop(0, SPAN, forward, 0)
-    w_step(2)
 
     top = mxb[0]
     for j in range(1, SPAN):
@@ -465,12 +493,11 @@
 
         @pl.when(i == 4)
         def _():
-            w_step(3)
+            w_step(2)
 
         return 0
 
     lax.fori_loop(0, SPAN, backward, 0)
-    w_step(4)
 
     key_t = jnp.concatenate([jnp.transpose(kvbuf[j, :, :HD]) for j in range(SPAN)], axis=1)
     for g in range(GROUP):
@@ -482,7 +509,7 @@
         dqbuf[:, g * HD:(g + 1) * HD] = jnp.transpose(grad_t) * SCALE
     dq_copy = remote(dqbuf.at[pl.ds((1 - core) * ROWS, ROWS)], dqrecv, dqs, dqr, sib, h)
     dq_copy.start()
-    w_step(5)
+    w_step(3)
 
     acc = ownbuf[...]
     ownbuf[...] = acc
@@ -515,13 +542,15 @@
 
     for k in range(1, 4):
         gx_copy(k, False).start()
+    w_step(4)
     dq_copy.wait_recv()
     gq_ref[...] = (dqbuf[own_rows, :] + dqrecv[...]).astype(jnp.bfloat16)
+    w_step(5)
     z_wait.wait_recv()
     for k in range(1, 4):
         gx_copy(k, True).start()
-
     w_step(6)
+
     own_delta.wait()
     for k in range(1, 4):
         del_wait(k).wait_recv()
@@ -597,19 +626,10 @@
 
     for k in range(1, 4):
         del_copy(k).wait_send()
-        ay_copy(k).wait_send()
-        by_copy(k).wait_send()
         gx_copy(k, False).wait_send()
         gx_copy(k, True).wait_send()
-    for k in range(1, 5):
-        for colour in range(2):
-            zp_copy(k, colour, False).wait_send()
-            if k < 4:
-                zm_copy(k, colour, False).wait_send()
-    for o in range(8):
-        fa_copy(o, core).wait_send()
-    for y_ in range(4):
-        fb_copy(y_, core).wait_send()
+    for build, args in sent:
+        build(*args).wait_send()
     dq_copy.wait_send()
     z_send.wait_send()
     for n, src, buf, ss, rs in (
@@ -619,6 +639,17 @@
     ):
         for k in range(1, n):
             remote(src, buf.at[0], ss.at[k], rs.at[k], s, h).wait_send()
+
+
+def finish(gq_in, gkv_in, tile_in, slot_ref, gq_out, gkv_out, sc_out):
+    gq_out[...] = gq_in[...]
+    gkv_out[...] = gkv_in[...]
+    tile = tile_in[...]
+    sub = lax.broadcasted_iota(jnp.int32, (8, 128), 0)
+    scores = jnp.zeros((8, 128), jnp.float32)
+    for i in range(8):
+        scores = jnp.where(sub == slot_ref[i], tile[i:i + 1], scores)
+    sc_out[...] = scores[:, :16]
 
 
 def on_device(queries, keyval, grad_out, doc_ids, deltas, node_weights, layer_slot):
@@ -658,7 +689,7 @@
     ]
     sems = [
         9, 9, 9, 9, 16, 16, None, None, 9, 9, None, None, 4, 4, 2,
-        4, 4, 5, 5, 4, 4, 5, 5, 4, 4, 4, 4, 8, 8, 4, 4, None, None, 8, 8,
+        4, 4, 40, 40, 10, 10, 16, 16, 8, 8, 64, None, None, None, 8, 8,
         8, 8, 8, 8, 4, 4,
     ]
     scratch += [D if n is None else D((n,)) for n in sems]
@@ -673,7 +704,7 @@
         out_specs=(vmem, vmem, vmem),
         scratch_shapes=scratch,
         compiler_params=pltpu.CompilerParams(
-            has_side_effects=True, vmem_limit_bytes=60 * 1024 * 1024
+            has_side_effects=True, collective_id=0, vmem_limit_bytes=60 * 1024 * 1024
         ),
     )(
         queries,
@@ -683,9 +714,16 @@
         deltas.reshape(128, 8192),
         node_weights.T,
     )
-    placing = (layer_slot[:, None] == jnp.arange(8, dtype=jnp.int32)[None, :]).astype(f32)
-    scores = jnp.dot(placing.T, tile[:, :16], precision=lax.Precision.HIGHEST)
-    return (grad_query, grad_keyval, scores)
+    return pl.pallas_call(
+        finish,
+        out_shape=(
+            jax.ShapeDtypeStruct((128, 1024), bf),
+            jax.ShapeDtypeStruct((128, 256), bf),
+            jax.ShapeDtypeStruct((8, 16), f32),
+        ),
+        in_specs=[vmem, vmem, vmem, pl.BlockSpec(memory_space=pltpu.SMEM)],
+        out_specs=(vmem, vmem, vmem),
+    )(grad_query, grad_keyval, tile, layer_slot)
 
 
 def solution(mesh):

time: 107 us -> 87.9 us (0.82); the launches traced: 107 us -> 86.3 us
  Pallas kernels: 101 us -> 85.7 us
  local copies, waits for them, and re-layouts: 3.14 us -> 0 us
  matrix products: 1.52 us -> 0 us
    pallas_call x1, Pallas kernels: 101 us -> 83.9 us  [on_device(): pl.pallas_call(kernel, out_shape=(jax.ShapeDtypeStruct((128, 1024), bf),...]
    unnamed x4 -> x0, local copies, waits for them, and re-layouts: 3.14 us -> none
    pallas_call x0 -> x1, Pallas kernels: none -> 1.73 us  [on_device(): pl.pallas_call(finish, out_shape=(jax.ShapeDtypeStruct((128, 1024), bf),...]
    dot_general x1 -> x0, matrix products: 1.52 us -> none  [on_device(): scores = jnp.dot(placing.T, tile[:, :16], precision=lax.Precision.HIGHEST)]
where the time goes in v2:
time: 87.9 us; the launch traced here: 86.3 us
  Pallas kernels  85.7 us (97%)
    pallas_call x1, Pallas kernels, on_device(): pl.pallas_call(kernel, out_shape=(jax.ShapeDtypeStruct((128, 1024), bf),...  83.9 us

profile of v2, /device:TPU:8, one launch (start us, length us, event | category | flops | bytes accessed | tf_op | source)
XLA Modules:
  0.0 86.3 jit_solution(18268711479430055144)
XLA Ops:
  0.6 83.9 %shard_map.94 = (bf16[128,1024]{1,0:T(8,128)(2,1)}, bf16[128,256]{1,0:T(8,128)(2,1)}, f32[8,128]{1,0:T(8,128)}) custom-call(bf16[128,1024]{1,0:T(8,128)(2,1)} %q_ref.1, bf16[128,256]{1,0:T(8,128)(2,1)} %kv_ref.1, bf16[128,1024]{1,0:T(8,128)(2,1)} %go_ref.1, s32[1,128]{1,0:T(1,128)} %bitcast.5, bf16[128,8192]{1,0:T(8,128)(2,1)} %bitcast.3, ...), custom_call_target="tpu_custom_call" | custom-call | tf_op jit(solution)/shard_map/pallas_call | solution.py:696
  84.6 1.7 %shard_map.95 = (bf16[128,1024]{1,0:T(8,128)(2,1)}, bf16[128,256]{1,0:T(8,128)(2,1)}, f32[8,16]{1,0:T(8,128)}) custom-call(bf16[128,1024]{1,0:T(8,128)(2,1)} %get-tuple-element.6.gq_in, bf16[128,256]{1,0:T(8,128)(2,1)} %get-tuple-element.7.gkv_in, f32[8,128]{1,0:T(8,128)} %get-tuple-element.8.tile_in, s32[8]{0:T(128)} %slot_ref.1), custom_call_target="tpu_custom_call" | custom-call | tf_op jit(solution)/shard_map/pallas_call | solution.py:717

commit v3 on v2

v3 whole, which is shorter than its diff:
```python
import math

import jax
import jax.numpy as jnp
from jax import lax
from jax.experimental import pallas as pl
from jax.experimental.pallas import tpu as pltpu
from jax.sharding import PartitionSpec as P

HD = 128
GROUP = 8
ROWS = 128
SPAN = 9
CUT = 16
FORWARD_STEPS = ((1, (0, 1)), (3, (2, 3)), (5, (4, 5)), (7, (6,)))
STEPS_1, STEPS_2, STEPS_3, STEPS_4, STEPS_5, STEPS_6 = (7, 8), (9,), (), (10, 11), (), (12,)
NEG = -1e30
FLOOR = -1e29
SCALE = 1.0 / math.sqrt(HD)
EXP_SCALE = SCALE * math.log2(math.e)
MESH = pl.DeviceIdType.MESH
NT = (((1,), (1,)), ((), ()))


def remote(src, dst, send, recv, seq, head):
    return pltpu.make_async_remote_copy(
        src_ref=src,
        dst_ref=dst,
        send_sem=send,
        recv_sem=recv,
        device_id=(seq, head),
        device_id_type=MESH,
    )


def kernel(
    q_ref,
    kv_ref,
    go_ref,
    doc_ref,
    del_ref,
    wt_ref,
    gq_ref,
    gkv_ref,
    sc_ref,
    qall,
    goall,
    kvbuf,
    docbuf,
    docq,
    bias,
    ebuf,
    dpbuf,
    mxb,
    lsb,
    dsb,
    stat,
    strecv,
    pbuf,
    dsbuf,
    sendbuf,
    dkvrecv,
    ownbuf,
    dqbuf,
    gqbuf,
    dqrecv,
    dbuf,
    wbuf,
    pbig,
    gbuf,
    arsrc,
    ar1,
    ar2,
    kvs,
    kvr,
    docs,
    docr,
    qs,
    qr,
    sts,
    str_,
    dks,
    dkr,
    dqs,
    dqr,
    dls,
    dlr,
    loc,
    ays,
    ayr,
    azs,
    azr,
    bzs,
    bzr,
    bys,
    byr,
    bos,
    bor,
    fs,
    fr,
    g1s,
    g1r,
    gxs,
    gxr,
    a1s,
    a1r,
    a2s,
    a2r,
):
    s = lax.axis_index("seq")
    h = lax.axis_index("head")
    core = lax.rem(s, 2)
    chip = s // 2
    zl = lax.rem(chip, 4)
    y = chip // 4
    zh = lax.rem(h, 2)
    x = h // 2
    z = zh * 4 + zl
    sib = s + 1 - 2 * core

    def at_yz(y_, z_, c_):
        return (y_ * 4 + lax.rem(z_, 4)) * 2 + c_, x * 2 + z_ // 4

    def kv_copy(j):
        return remote(kv_ref, kvbuf.at[j], kvs.at[j], kvr.at[j], lax.rem(s + 2 * j, 32), h)

    def doc_copy(j):
        return remote(doc_ref, docbuf.at[j], docs.at[j], docr.at[j], lax.rem(s + 2 * j, 32), h)

    own_rows = pl.ds(core * ROWS, ROWS)
    far_rows = pl.ds((1 - core) * ROWS, ROWS)
    q_copy = remote(q_ref, qall.at[own_rows], qs.at[0], qr.at[0], sib, h)
    q_wait = remote(q_ref, qall.at[far_rows], qs.at[0], qr.at[0], sib, h)
    go_copy = remote(go_ref, goall.at[own_rows], qs.at[1], qr.at[1], sib, h)
    go_wait = remote(go_ref, goall.at[far_rows], qs.at[1], qr.at[1], sib, h)
    own = [
        pltpu.make_async_copy(src, dst, loc.at[2 + n])
        for n, (src, dst) in enumerate(
            (
                (q_ref, qall.at[own_rows]),
                (go_ref, goall.at[own_rows]),
                (kv_ref, kvbuf.at[0]),
                (doc_ref, docbuf.at[0]),
                (doc_ref, docq.at[core]),
            )
        )
    ]
    for copy in own:
        copy.start()

    barrier = pltpu.get_barrier_semaphore()

    def greet(seq, head):
        pl.semaphore_signal(barrier, inc=1, device_id=(seq, head), device_id_type=MESH)

    for k in range(1, 16):
        greet(lax.rem(s + 2 * k, 32), h)
    for k in range(4):
        greet(lax.rem(y + k, 4) * 8 + zl * 2 + 1 - core, h)
        greet(y * 8 + k * 2 + core, x * 2 + 1 - zh)
    for k in range(1, 4):
        for n in range(4):
            for c_ in range(2):
                greet((n * 4 + zl) * 2 + c_, lax.rem(x + k, 4) * 2 + zh)
    pl.semaphore_wait(barrier, 47)

    LA, LB = pl.ds(0, CUT), pl.ds(CUT, 64 - CUT)
    sent = {}

    def send(build, *args):
        build(*args).start()
        sent[(build, args)] = True

    def piece(r, m, rows, c_=None):
        o = lax.rem(z + r, 8)
        return wbuf.at[
            o // 4, lax.rem(y + 4 - m, 4), lax.rem(o, 4), core if c_ is None else c_, rows
        ]

    def to_y(k):
        return at_yz(lax.rem(y + k, 4), z, core)

    def to_z(d):
        return at_yz(y, lax.rem(z + d + 8, 8), core)

    def ay(k, wait=False):
        dst = piece(0, k if wait else 0, LA)
        return remote(wt_ref.at[LA], dst, ays.at[k], ayr.at[k], *to_y(k))

    def az(d, k, half, wait=False):
        o = lax.rem(z + (-d * (k if wait else k - 1)) % 8, 8)
        ref = wbuf.at[o // 4, pl.ds(half * 2, 2), lax.rem(o, 4), core, LA]
        n = ((d < 0) * 5 + k) * 2 + half
        return remote(ref, ref, azs.at[n], azr.at[n], *to_z(d))

    def bz(d, k, wait=False):
        ref = piece((-d * (k if wait else k - 1)) % 8, 0, LB)
        src = wt_ref.at[LB] if k == 1 else ref
        n = (d < 0) * 5 + k
        return remote(src, ref, bzs.at[n], bzr.at[n], *to_z(d))

    def by(d, r, wait=False):
        ref = piece(r, (d % 4) if wait else 0, LB)
        src = wt_ref.at[LB] if r == 0 else ref
        n = (d < 0) * 8 + r
        return remote(src, ref, bys.at[n], byr.at[n], *to_y(d % 4))

    def bo(d, r, wait=False):
        ref = piece(r, 2 if wait else d % 4, LB)
        return remote(ref, ref, bos.at[r], bor.at[r], *to_y(d % 4))

    def fa(r):
        o = lax.rem(z + r, 8)
        ref = wbuf.at[o // 4, :, lax.rem(o, 4), core, LA]
        return remote(ref, ref, fs.at[r], fr.at[0], sib, h)

    def fb(m):
        ref = wbuf.at[:, lax.rem(y + 4 - m, 4), :, core, LB]
        return remote(ref, ref, fs.at[8 + m], fr.at[1 + m // 2 + m % 2], sib, h)

    def fb_one(r):
        ref = piece(r, 2, LB)
        return remote(ref, ref, fs.at[16 + r], fr.at[4], sib, h)

    own_w = pltpu.make_async_copy(wt_ref, wbuf.at[zh, y, zl, core], loc.at[1])
    own_w.start()
    for d in (1, -1):
        send(bz, d, 1)
    for k in (1, 3, 2):
        send(ay, k)
    for d in (1, -1):
        send(by, d, 0)
    STEPS = {1: 4, -1: 3}

    def a_ring(k):
        for half in range(2):
            for d in (1, -1):
                if k <= STEPS[d]:
                    az(d, k, half, True).wait_recv()
                    if k < STEPS[d]:
                        send(az, d, k + 1, half)
        for r in sorted({k, -k % 8}):
            send(fa, r)

    def b_ring(k):
        for d in (1, -1):
            if k <= STEPS[d]:
                bz(d, k, True).wait_recv()
                if k < STEPS[d]:
                    send(bz, d, k + 1)
                r = (-d * k) % 8
                send(by, 1, r)
                send(by, -1, r)
        if k == 4:
            send(fb, 0)

    def b_side(k):
        for r in sorted({k, -k % 8}):
            for d in (1, -1):
                by(d, r, True).wait_recv()
                if (d > 0) == (r < 4):
                    send(bo, d, r)
        if k == 4:
            send(fb, 1)
            send(fb, 3)

    def b_far(k):
        for r in sorted({k, -k % 8}):
            bo(1 if r < 4 else -1, r, True).wait_recv()
            send(fb_one, r)

    def a_side():
        own_w.wait()
        for k in (1, 3, 2):
            ay(k, True).wait_recv()
        for half in range(2):
            send(az, 1, 1, half)
            send(az, -1, 1, half)
        send(fa, 0)

    plan = (
        ((b_ring, 1), (a_side,)),
        ((b_side, 0),),
        ((b_ring, 2),),
        ((a_ring, 1),),
        ((b_side, 1), (b_far, 0)),
        ((b_ring, 3),),
        ((a_ring, 2),),
        ((b_side, 2), (b_far, 1)),
        ((b_ring, 4),),
        ((a_ring, 3),),
        ((b_side, 3), (b_far, 2)),
        ((a_ring, 4), (b_side, 4), (b_far, 3)),
        ((b_far, 4),),
    )

    def w_step(*ns):
        for n in ns:
            for job in plan[n]:
                job[0](*job[1:])

    def w_near():
        ref = wbuf.at[:, :, :, 1 - core, LA]
        remote(ref, ref, fs.at[0], fr.at[0], sib, h).wait_recv()
        for m in (0, 1, 3):
            ref = wbuf.at[:, lax.rem(y + 4 - m, 4), :, 1 - core, LB]
            remote(ref, ref, fs.at[0], fr.at[1 + m // 2 + m % 2], sib, h).wait_recv()

    def w_far():
        ref = wbuf.at[:, lax.rem(y + 2, 4), :, 1 - core, LB]
        remote(ref, ref, fs.at[0], fr.at[4], sib, h).wait_recv()

    docq_send = remote(doc_ref, docq.at[core], docs.at[0], docr.at[0], sib, h)
    docq_wait = remote(doc_ref, docq.at[1 - core], docs.at[0], docr.at[0], sib, h)
    docq_send.start()
    for j in range(1, SPAN):

        @pl.when(chip + j <= 15)
        def _():
            doc_copy(j).start()
            kv_copy(j).start()

    q_copy.start()
    go_copy.start()

    def del_copy(k):
        xt = lax.rem(x + k, 4)
        return remote(
            del_ref.at[:, pl.ds(xt * 2048, 2048)],
            dbuf.at[x],
            dls.at[k],
            dlr.at[k],
            s,
            xt * 2 + zh,
        )

    def del_wait(k):
        xf = lax.rem(x + 4 - k, 4)
        return remote(
            del_ref.at[:, pl.ds(xf * 2048, 2048)],
            dbuf.at[xf],
            dls.at[k],
            dlr.at[k],
            s,
            xf * 2 + zh,
        )

    for k in range(1, 4):
        del_copy(k).start()
    own_delta = pltpu.make_async_copy(
        del_ref.at[:, pl.ds(x * 2048, 2048)], dbuf.at[x], loc.at[0]
    )
    own_delta.start()

    for j in range(SPAN):

        @pl.when(chip < j)
        def _():
            mxb[j] = jnp.full((8, 2048), FLOOR, jnp.float32)
            lsb[j] = jnp.zeros((8, 2048), jnp.float32)
            dsb[j] = jnp.zeros((8, 2048), jnp.float32)
            kvbuf[j] = jnp.zeros((ROWS, 256), jnp.bfloat16)
            dsbuf[j] = jnp.zeros((ROWS, 2048), jnp.bfloat16)

    for copy in own:
        copy.wait()
    docq_wait.wait_recv()
    q_wait.wait_recv()
    go_wait.wait_recv()

    def forward(j, _):
        @pl.when(chip >= j)
        def _():
            @pl.when(j > 0)
            def _():
                doc_copy(j).wait_recv()
                kv_copy(j).wait_recv()

            ids = docbuf[j]
            drow = jnp.concatenate((docq[0], docq[1]), axis=1)
            low = jnp.zeros((1, 256), jnp.float32)
            for v in range(3):
                count = jnp.sum((ids == v).astype(jnp.float32), axis=1, keepdims=True)
                low = low + jnp.where(drow > v, count, 0.0)
            place = lax.broadcasted_iota(jnp.int32, (ROWS, 256), 0)
            token = lax.broadcasted_iota(jnp.int32, (ROWS, 256), 1)
            high = jnp.where(j == 0, token - core * ROWS, ROWS)
            keep = (place >= low.astype(jnp.int32)) & (place <= high)
            bias[...] = jnp.where(keep, 0.0, NEG)
            key_rows = kvbuf[j, :, :HD]
            value_rows = kvbuf[j, :, HD:]
            for g in range(GROUP):
                cols = slice(g * 256, (g + 1) * 256)
                logits = lax.dot_general(
                    key_rows, qall[:, g * HD:(g + 1) * HD], NT, preferred_element_type=jnp.float32
                )
                grad_p = lax.dot_general(
                    value_rows, goall[:, g * HD:(g + 1) * HD], NT, preferred_element_type=jnp.float32
                )
                logits = logits + bias[...]
                top = jnp.maximum(jnp.max(logits, axis=0, keepdims=True), FLOOR)
                weight = jnp.exp2((logits - top) * EXP_SCALE)
                ebuf[j, :, cols] = weight
                dpbuf[j, :, cols] = grad_p
                mxb[j, :, cols] = jnp.broadcast_to(top, (8, 256))
                lsb[j, :, cols] = jnp.sum(weight.reshape(16, 8, 256), axis=0)
                dsb[j, :, cols] = jnp.sum((weight * grad_p).reshape(16, 8, 256), axis=0)

        for n, ns in FORWARD_STEPS:

            @pl.when(j == n)
            def _():
                w_step(*ns)

        return 0

    lax.fori_loop(0, SPAN, forward, 0)

    top = mxb[0]
    for j in range(1, SPAN):
        top = jnp.maximum(top, mxb[j])
    total = jnp.zeros((8, 2048), jnp.float32)
    dots = jnp.zeros((8, 2048), jnp.float32)
    for j in range(SPAN):
        factor = jnp.exp2((mxb[j] - top) * EXP_SCALE)
        total = total + factor * lsb[j]
        dots = dots + factor * dsb[j]
    total = jnp.sum(total, axis=0, keepdims=True)
    dots = jnp.sum(dots, axis=0, keepdims=True)
    row = lax.broadcasted_iota(jnp.int32, (8, 2048), 0)
    stat[...] = jnp.where(row == 0, top, jnp.where(row == 1, total, dots))
    stat_copy = remote(stat, strecv, sts, str_, sib, h)
    stat_copy.start()
    w_step(*STEPS_1)
    stat_copy.wait_recv()
    m_own, m_far = stat[0:1], strecv[0:1]
    m_all = jnp.maximum(m_own, m_far)
    f_own = jnp.exp2((m_own - m_all) * EXP_SCALE)
    f_far = jnp.exp2((m_far - m_all) * EXP_SCALE)
    l_all = stat[1:2] * f_own + strecv[1:2] * f_far
    d_all = (stat[2:3] * f_own + strecv[2:3] * f_far) / l_all
    stat_copy.wait_send()
    stat[0:1] = m_all
    stat[1:2] = 1.0 / l_all
    stat[2:3] = d_all

    def dk_copy(j):
        return remote(
            sendbuf.at[j], dkvrecv.at[j], dks.at[j], dkr.at[j], lax.rem(s - 2 * j + 32, 32), h
        )

    def backward(i, _):
        j = SPAN - 1 - i

        @pl.when(chip >= j)
        def _():
            for g in range(GROUP):
                cols = slice(g * 256, (g + 1) * 256)
                factor = jnp.exp2((mxb[j, 0:1, cols] - stat[0:1, cols]) * EXP_SCALE)
                factor = factor * stat[1:2, cols]
                probs = ebuf[j, :, cols] * factor
                pbuf[:, cols] = probs.astype(jnp.bfloat16)
                grad_l = probs * (dpbuf[j, :, cols] - stat[2:3, cols])
                dsbuf[j, :, cols] = grad_l.astype(jnp.bfloat16)
            grad_k = jnp.zeros((ROWS, HD), jnp.float32)
            grad_v = jnp.zeros((ROWS, HD), jnp.float32)
            for g in range(GROUP):
                cols, head = slice(g * 256, (g + 1) * 256), slice(g * HD, (g + 1) * HD)
                grad_k = grad_k + jnp.dot(
                    dsbuf[j, :, cols], qall[:, head], preferred_element_type=jnp.float32
                )
                grad_v = grad_v + jnp.dot(
                    pbuf[:, cols], goall[:, head], preferred_element_type=jnp.float32
                )
            grad_k = grad_k * SCALE
            ownbuf[:, :HD] = grad_k
            ownbuf[:, HD:] = grad_v

            @pl.when(j > 0)
            def _():
                sendbuf[j, :, :HD] = grad_k.astype(jnp.bfloat16)
                sendbuf[j, :, HD:] = grad_v.astype(jnp.bfloat16)
                dk_copy(j).start()

        return 0

    lax.fori_loop(0, SPAN, backward, 0)
    w_step(*STEPS_2)

    key_t = jnp.concatenate([jnp.transpose(kvbuf[j, :, :HD]) for j in range(SPAN)], axis=1)
    for g in range(GROUP):
        grad_t = jnp.dot(
            key_t,
            dsbuf[:, :, g * 256:(g + 1) * 256].reshape(SPAN * ROWS, 256),
            preferred_element_type=jnp.float32,
        )
        dqbuf[:, g * HD:(g + 1) * HD] = jnp.transpose(grad_t) * SCALE
    dq_copy = remote(dqbuf.at[pl.ds((1 - core) * ROWS, ROWS)], dqrecv, dqs, dqr, sib, h)
    dq_copy.start()
    w_step(*STEPS_3)

    acc = ownbuf[...]
    ownbuf[...] = acc
    for j in range(1, SPAN):

        @pl.when(chip + j <= 15)
        def _():
            dk_copy(j).wait_recv()
            ownbuf[...] += dkvrecv[j].astype(jnp.float32)

    grad_kv = ownbuf[...].astype(jnp.bfloat16)
    gbuf[h] = grad_kv
    out_kv = pltpu.make_async_copy(gbuf.at[h], gkv_ref, loc.at[7])
    out_kv.start()

    z_send = remote(gbuf.at[h], gbuf.at[h], g1s, g1r, s, x * 2 + 1 - zh)
    z_wait = remote(gbuf.at[h], gbuf.at[x * 2 + 1 - zh], g1s, g1r, s, x * 2 + 1 - zh)
    z_send.start()

    def gx_copy(k, far):
        hh = (x * 2 + 1 - zh) if far else h
        xt = lax.rem(x + k, 4)
        n = k + (4 if far else 0)
        return remote(gbuf.at[hh], gbuf.at[hh], gxs.at[n], gxr.at[n], s, xt * 2 + zh)

    def gx_wait(k, far):
        xf = lax.rem(x + 4 - k, 4)
        hh = xf * 2 + ((1 - zh) if far else zh)
        n = k + (4 if far else 0)
        return remote(gbuf.at[hh], gbuf.at[hh], gxs.at[n], gxr.at[n], s, h)

    for k in range(1, 4):
        gx_copy(k, False).start()
    w_step(*STEPS_4)
    dq_copy.wait_recv()
    gqbuf[...] = (dqbuf[own_rows, :] + dqrecv[...]).astype(jnp.bfloat16)
    out_q = pltpu.make_async_copy(gqbuf, gq_ref, loc.at[8])
    out_q.start()
    w_step(*STEPS_5)
    z_wait.wait_recv()
    for k in range(1, 4):
        gx_copy(k, True).start()

    own_delta.wait()
    for k in range(1, 4):
        del_wait(k).wait_recv()
    def project(n):
        out = None
        for b in range(2):
            left = dbuf[:, :, b * 1024:(b + 1) * 1024].reshape(512, 1024)
            right = wbuf[b, n].reshape(512, 1024)
            part = lax.dot_general(left, right, NT, preferred_element_type=jnp.float32)
            out = part if out is None else out + part
        pbig[n] = out

    w_near()

    def near(k, _):
        project(lax.rem(y + 3 + k, 4))
        return 0

    lax.fori_loop(0, 3, near, 0)
    w_step(*STEPS_6)
    w_far()
    project(lax.rem(y + 2, 4))
    for k in range(1, 4):
        gx_wait(k, False).wait_recv()
        gx_wait(k, True).wait_recv()

    lane = lax.broadcasted_iota(jnp.int32, (8, 128), 1)
    sub = lax.broadcasted_iota(jnp.int32, (8, 128), 0)
    tile = jnp.zeros((8, 128), jnp.float32)
    for hh in range(8):
        grads = gbuf[hh].astype(jnp.float32)
        off = (hh % 2) * 256
        for i in range(4):
            prod = pbig[hh // 2, i * 128:(i + 1) * 128, off:off + 256] * grads
            prod = jnp.sum(prod.reshape(16, 8, 256), axis=0)
            prod = jnp.sum(prod, axis=0, keepdims=True)
            for n in range(2):
                value = jnp.sum(prod[:, n * 128:(n + 1) * 128], axis=1, keepdims=True)
                hit = (sub == 2 * i + zh) & (lane == 2 * hh + n)
                tile = jnp.where(hit, value, tile)
    tile = tile * (1.0 / 64.0)

    ring4, ring8 = (2, 1, 3, 0), (4, 3, 5, 2, 6, 1, 7, 0)
    plane = [(dx, dy, dc) for dx in ring4 for dy in ring4 for dc in (1, 0)][:-1]
    plane.sort(key=lambda o: -(min(o[0], 4 - o[0]) + min(o[1], 4 - o[1])))

    me = x * 8 + y * 2 + core

    def plane_copy(dx, dy, dc, wait=False):
        n = dx * 8 + dy * 2 + dc
        slot = me
        if wait:
            slot = lax.rem(x + 4 - dx, 4) * 8 + lax.rem(y + 4 - dy, 4) * 2
            slot = slot + lax.rem(core + dc, 2)
        c_ = lax.rem(core + dc, 2)
        seq = (lax.rem(y + dy, 4) * 4 + zl) * 2 + c_
        head = lax.rem(x + dx, 4) * 2 + zh
        return remote(arsrc.at[0], ar1.at[slot], a1s.at[n], a1r.at[n], seq, head)

    def z_copy(dz, wait=False):
        slot = lax.rem(z + 8 - dz, 8) if wait else z
        seq, head = at_yz(y, lax.rem(z + dz, 8), core)
        return remote(arsrc.at[1], ar2.at[slot], a2s.at[dz], a2r.at[dz], seq, head)

    arsrc[0] = tile
    for offset in plane:
        plane_copy(*offset).start()
    for offset in reversed(plane):
        plane_copy(*offset, True).wait_recv()
    ar1[me] = tile
    tile = jnp.sum(ar1[...], axis=0)
    arsrc[1] = tile
    for dz in ring8[:-1]:
        z_copy(dz).start()
    for dz in reversed(ring8[:-1]):
        z_copy(dz, True).wait_recv()
    ar2[z] = tile
    tile = jnp.sum(ar2[...], axis=0)
    sc_ref[...] = tile

    out_kv.wait()
    out_q.wait()
    docq_send.wait_send()
    q_copy.wait_send()
    go_copy.wait_send()
    for j in range(1, SPAN):

        @pl.when(chip + j <= 15)
        def _():
            doc_copy(j).wait_send()
            kv_copy(j).wait_send()

        @pl.when(chip >= j)
        def _():
            dk_copy(j).wait_send()

    for k in range(1, 4):
        del_copy(k).wait_send()
        gx_copy(k, False).wait_send()
        gx_copy(k, True).wait_send()
    for build, args in sent:
        build(*args).wait_send()
    dq_copy.wait_send()
    z_send.wait_send()
    for offset in plane:
        plane_copy(*offset).wait_send()
    for dz in ring8[:-1]:
        z_copy(dz).wait_send()


def finish(gq_in, gkv_in, tile_in, slot_ref, gq_out, gkv_out, sc_out):
    gq_out[...] = gq_in[...]
    gkv_out[...] = gkv_in[...]
    tile = tile_in[...]
    sub = lax.broadcasted_iota(jnp.int32, (8, 128), 0)
    scores = jnp.zeros((8, 128), jnp.float32)
    for i in range(8):
        scores = jnp.where(sub == slot_ref[i], tile[i:i + 1], scores)
    sc_out[...] = scores[:, :16]


def on_device(queries, keyval, grad_out, doc_ids, deltas, node_weights, layer_slot):
    vmem = pl.BlockSpec(memory_space=pltpu.VMEM)
    hbm = pl.BlockSpec(memory_space=pl.ANY)
    bf, f32, i32 = jnp.bfloat16, jnp.float32, jnp.int32
    V, D = pltpu.VMEM, pltpu.SemaphoreType.DMA
    scratch = [
        V((256, 1024), bf),
        V((256, 1024), bf),
        V((SPAN, 128, 256), bf),
        V((SPAN, 1, 128), i32),
        V((2, 1, 128), i32),
        V((128, 256), f32),
        V((SPAN, 128, 2048), f32),
        V((SPAN, 128, 2048), f32),
        V((SPAN, 8, 2048), f32),
        V((SPAN, 8, 2048), f32),
        V((SPAN, 8, 2048), f32),
        V((8, 2048), f32),
        V((8, 2048), f32),
        V((128, 2048), bf),
        V((SPAN, 128, 2048), bf),
        V((SPAN, 128, 256), bf),
        V((SPAN, 128, 256), bf),
        V((128, 256), f32),
        V((256, 1024), f32),
        V((128, 1024), bf),
        V((128, 1024), f32),
        V((4, 128, 2048), bf),
        V((2, 4, 4, 2, 64, 1024), bf),
        V((4, 512, 512), f32),
        V((8, 128, 256), bf),
        V((2, 8, 128), f32),
        V((32, 8, 128), f32),
        V((8, 8, 128), f32),
    ]
    sems = [
        9, 9, 9, 9, 2, 2, None, None, 9, 9, None, None, 4, 4, 9,
        4, 4, 20, 20, 10, 10, 16, 16, 8, 8, 24, 5, None, None, 8, 8,
        32, 32, 8, 8,
    ]
    scratch += [D if n is None else D((n,)) for n in sems]
    grad_query, grad_keyval, tile = pl.pallas_call(
        kernel,
        out_shape=(
            jax.ShapeDtypeStruct((128, 1024), bf),
            jax.ShapeDtypeStruct((128, 256), bf),
            jax.ShapeDtypeStruct((8, 128), f32),
        ),
        in_specs=[hbm, hbm, hbm, hbm, hbm, hbm],
        out_specs=(hbm, hbm, vmem),
        scratch_shapes=scratch,
        compiler_params=pltpu.CompilerParams(
            has_side_effects=True, collective_id=0, vmem_limit_bytes=60 * 1024 * 1024
        ),
    )(
        queries,
        keyval,
        grad_out,
        doc_ids.reshape(1, 128),
        deltas.reshape(128, 8192),
        node_weights.T,
    )
    return pl.pallas_call(
        finish,
        out_shape=(
            jax.ShapeDtypeStruct((128, 1024), bf),
            jax.ShapeDtypeStruct((128, 256), bf),
            jax.ShapeDtypeStruct((8, 16), f32),
        ),
        in_specs=[vmem, vmem, vmem, pl.BlockSpec(memory_space=pltpu.SMEM)],
        out_specs=(vmem, vmem, vmem),
    )(grad_query, grad_keyval, tile, layer_slot)


def solution(mesh):
    return jax.shard_map(
        on_device,
        mesh=mesh,
        in_specs=(
            P("seq", "head"),
            P("seq", "head"),
            P("seq", "head"),
            P("seq"),
            P("head", "seq", None),
            P("head", "seq"),
            P(),
        ),
        out_specs=(P("seq", "head"), P("seq", "head"), P()),
        check_vma=False,
    )
```

time: 87.9 us -> 82.7 us (0.941)
  Pallas kernels: 85.7 us -> 80.6 us
    pallas_call x1, Pallas kernels: 83.9 us -> 78.9 us  [on_device(): pl.pallas_call(kernel, out_shape=(jax.ShapeDtypeStruct((128, 1024), bf),...]
where the time goes in v3:
time: 82.7 us; the launch traced here: 81.2 us
  Pallas kernels  80.6 us (97%)
    pallas_call x1, Pallas kernels, on_device(): pl.pallas_call(kernel, out_shape=(jax.ShapeDtypeStruct((128, 1024), bf),...  78.9 us
    pallas_call x1, Pallas kernels, on_device(): pl.pallas_call(finish, out_shape=(jax.ShapeDtypeStruct((128, 1024), bf),...  1.73 us

profile of v3, /device:TPU:8, one launch (start us, length us, event | category | flops | bytes accessed | tf_op | source)
XLA Modules:
  0.0 81.2 jit_solution(3998374769653526675)
XLA Ops:
  0.6 78.9 %shard_map.94 = (bf16[128,1024]{1,0:T(8,128)(2,1)}, bf16[128,256]{1,0:T(8,128)(2,1)}, f32[8,128]{1,0:T(8,128)}) custom-call(bf16[128,1024]{1,0:T(8,128)(2,1)} %q_ref.1, bf16[128,256]{1,0:T(8,128)(2,1)} %kv_ref.1, bf16[128,1024]{1,0:T(8,128)(2,1)} %go_ref.1, s32[1,128]{1,0:T(1,128)} %bitcast.5, bf16[128,8192]{1,0:T(8,128)(2,1)} %bitcast.3, ...), custom_call_target="tpu_custom_call" | custom-call | tf_op jit(solution)/shard_map/pallas_call | solution.py:706
  79.5 1.7 %shard_map.95 = (bf16[128,1024]{1,0:T(8,128)(2,1)}, bf16[128,256]{1,0:T(8,128)(2,1)}, f32[8,16]{1,0:T(8,128)}) custom-call(bf16[128,1024]{1,0:T(8,128)(2,1)} %get-tuple-element.6.gq_in, bf16[128,256]{1,0:T(8,128)(2,1)} %get-tuple-element.7.gkv_in, f32[8,128]{1,0:T(8,128)} %get-tuple-element.8.tile_in, s32[8]{0:T(128)} %slot_ref.1), custom_call_target="tpu_custom_call" | custom-call | tf_op jit(solution)/shard_map/pallas_call | solution.py:727

commit v4 on v3

--- a/solution.py
+++ b/solution.py
@@ -608,6 +608,32 @@
     arsrc[0] = tile
     for offset in plane:
         plane_copy(*offset).start()
+
+    out_kv.wait()
+    out_q.wait()
+    docq_send.wait_send()
+    q_copy.wait_send()
+    go_copy.wait_send()
+    for j in range(1, SPAN):
+
+        @pl.when(chip + j <= 15)
+        def _():
+            doc_copy(j).wait_send()
+            kv_copy(j).wait_send()
+
+        @pl.when(chip >= j)
+        def _():
+            dk_copy(j).wait_send()
+
+    for k in range(1, 4):
+        del_copy(k).wait_send()
+        gx_copy(k, False).wait_send()
+        gx_copy(k, True).wait_send()
+    for build, args in sent:
+        build(*args).wait_send()
+    dq_copy.wait_send()
+    z_send.wait_send()
+
     for offset in reversed(plane):
         plane_copy(*offset, True).wait_recv()
     ar1[me] = tile
@@ -621,30 +647,6 @@
     tile = jnp.sum(ar2[...], axis=0)
     sc_ref[...] = tile
 
-    out_kv.wait()
-    out_q.wait()
-    docq_send.wait_send()
-    q_copy.wait_send()
-    go_copy.wait_send()
-    for j in range(1, SPAN):
-
-        @pl.when(chip + j <= 15)
-        def _():
-            doc_copy(j).wait_send()
-            kv_copy(j).wait_send()
-
-        @pl.when(chip >= j)
-        def _():
-            dk_copy(j).wait_send()
-
-    for k in range(1, 4):
-        del_copy(k).wait_send()
-        gx_copy(k, False).wait_send()
-        gx_copy(k, True).wait_send()
-    for build, args in sent:
-        build(*args).wait_send()
-    dq_copy.wait_send()
-    z_send.wait_send()
     for offset in plane:
         plane_copy(*offset).wait_send()
     for dz in ring8[:-1]:

time: 82.7 us -> 82.5 us (level)
  no operation moved by 1% of the time
where the time goes in v4:
time: 82.5 us; the launch traced here: 81.1 us
  Pallas kernels  80.4 us (97%)
    pallas_call x1, Pallas kernels, on_device(): pl.pallas_call(kernel, out_shape=(jax.ShapeDtypeStruct((128, 1024), bf),...  78.7 us
    pallas_call x1, Pallas kernels, on_device(): pl.pallas_call(finish, out_shape=(jax.ShapeDtypeStruct((128, 1024), bf),...  1.73 us

profile of v4, /device:TPU:8, one launch (start us, length us, event | category | flops | bytes accessed | tf_op | source)
XLA Modules:
  0.0 81.1 jit_solution(3329205830730538148)
XLA Ops:
  0.6 78.7 %shard_map.94 = (bf16[128,1024]{1,0:T(8,128)(2,1)}, bf16[128,256]{1,0:T(8,128)(2,1)}, f32[8,128]{1,0:T(8,128)}) custom-call(bf16[128,1024]{1,0:T(8,128)(2,1)} %q_ref.1, bf16[128,256]{1,0:T(8,128)(2,1)} %kv_ref.1, bf16[128,1024]{1,0:T(8,128)(2,1)} %go_ref.1, s32[1,128]{1,0:T(1,128)} %bitcast.5, bf16[128,8192]{1,0:T(8,128)(2,1)} %bitcast.3, ...), custom_call_target="tpu_custom_call" | custom-call | tf_op jit(solution)/shard_map/pallas_call | solution.py:708
  79.3 1.7 %shard_map.95 = (bf16[128,1024]{1,0:T(8,128)(2,1)}, bf16[128,256]{1,0:T(8,128)(2,1)}, f32[8,16]{1,0:T(8,128)}) custom-call(bf16[128,1024]{1,0:T(8,128)(2,1)} %get-tuple-element.6.gq_in, bf16[128,256]{1,0:T(8,128)(2,1)} %get-tuple-element.7.gkv_in, f32[8,128]{1,0:T(8,128)} %get-tuple-element.8.tile_in, s32[8]{0:T(128)} %slot_ref.1), custom_call_target="tpu_custom_call" | custom-call | tf_op jit(solution)/shard_map/pallas_call | solution.py:729
